TPU v7x, 512 devices: a whole 4x4x16 slice. The times are simulated.
512 devices in a mesh: clu: 64 (over x, z), grp: 8 (over y, core).
Axes of the slice: x: 4, y: 4, z: 16, core: 2. Of those that a mesh axis runs over, the one named last changes fastest.
Arguments:
- embeddings: bfloat16 [65536, 512], P(('clu', 'grp')), may hold values from -60 to 60
- cluster_id: int32 [65536], P(('clu', 'grp')), may hold values from 0 to 255, as said below
- cluster_group: int32 [256], replicated, may hold values from 0 to 63, as said below
Outputs:
- best_similarity: float32 [65536], P(('clu', 'grp'))
Inputs may be any that keep to these rules, and one draw needn't show every extreme that they name: `cluster_id`: on every device's rows, at most 8 rows belong to clusters of one group, and exactly 8 for some group. `cluster_group`: every group is named by exactly 4 clusters.
All inputs are finite; a program needn't handle non-finite values.
Results may differ from a plain program's by a relative error of at most 0.0015.
Values may be sent and summed in bfloat16 or wider, within the bound.
A program may use at most 64 MiB of HBM per device.

v0:
```python
import jax
import jax.numpy as jnp
from jax import lax
from jax.sharding import PartitionSpec as P


def normalize(embeddings):
    values = embeddings.astype(jnp.float32)
    scale = lax.rsqrt(jnp.sum(values * values, axis=-1, keepdims=True) + 1e-06)
    return (values * scale).astype(jnp.bfloat16)


def tile_max(best, queries, query_cl, query_pos, keys, key_cl, key_pos):
    sims = lax.dot_general(
        queries, keys, (((1,), (1,)), ((), ())), preferred_element_type=jnp.float32
    )
    score = jnp.where(query_cl[:, None] == key_cl[None, :], sims, 0.5 * sims)
    mask = (key_cl[None, :] >= 0) & (key_pos[None, :] < query_pos[:, None])
    return jnp.maximum(best, jnp.max(jnp.where(mask, score, -1.0), axis=1))


def shards(embeddings, cluster_id, cluster_group):
    rows, width = embeddings.shape
    n_clu = lax.axis_size("clu")
    slots = 4 * rows // n_clu
    block = slots * n_clu
    clusters = cluster_group.shape[0]
    unit = normalize(embeddings)
    table = cluster_id[:, None] == jnp.arange(clusters, dtype=jnp.int32)[None, :]
    dest = jnp.sum(jnp.where(table, cluster_group[None, :], 0), axis=1)
    dest_hot = (dest[:, None] == jnp.arange(n_clu, dtype=jnp.int32)[None, :]).astype(jnp.int32)
    position = jnp.sum(jnp.cumsum(dest_hot, axis=0) * dest_hot, axis=1) - 1
    send_units = jnp.zeros((n_clu, slots, width), jnp.bfloat16).at[dest, position].set(unit)
    send_clusters = jnp.full((n_clu, slots), -1, jnp.int32).at[dest, position].set(cluster_id)
    recv_units, recv_clusters = (
        lax.all_to_all(send_units, "clu", split_axis=0, concat_axis=0, tiled=True),
        lax.all_to_all(send_clusters, "clu", split_axis=0, concat_axis=0, tiled=True),
    )
    queries = recv_units.reshape(block, width)
    query_cl = recv_clusters.reshape(block)
    mine = lax.axis_index("grp")
    query_pos = mine * block + jnp.arange(block, dtype=jnp.int32)
    initial = jnp.full((block,), -1.0, jnp.float32)
    keys = lax.all_gather(queries, "grp", axis=0, tiled=True)
    key_cl = lax.all_gather(query_cl, "grp", axis=0, tiled=True)
    count = keys.shape[0]
    key_pos = jnp.arange(count, dtype=jnp.int32)

    def work(carry):
        return tile_max(carry, queries, query_cl, query_pos, keys, key_cl, key_pos)

    best = lax.cond(jnp.int32(0) < mine * block + block, work, lambda carry: carry, initial)
    returned = lax.all_to_all(
        best.reshape(n_clu, slots), "clu", split_axis=0, concat_axis=0, tiled=True
    )
    return returned[dest, position]


def solution(mesh):
    placed = (P(("clu", "grp"), None), P(("clu", "grp")), P())
    return jax.shard_map(
        shards, mesh=mesh, in_specs=placed, out_specs=P(("clu", "grp")), check_vma=False
    )
```

profile of v0, /device:TPU:1, one launch (start us, length us, event | category | flops | bytes accessed | tf_op | source)
XLA Modules:
  0.0 144.2 jit_solution(6819595550657814609)
XLA Ops:
  6.5 0.0 copy-start
  6.5 0.0 all-gather.3.cloned.1.call-start
  6.5 1.0 fusion.2
  7.6 0.9 select_reduce_fusion
  8.4 0.1 fusion.4
  8.5 0.2 reduce_window_sum.11
  8.7 0.2 select_reduce_fusion.1
  8.9 1.0 fusion.3
  10.0 7.1 %scatter_fusion.1 = bf16[64,8,512]{2,1,0:T(8,128)(2,1)S(1)} fusion(bf16[64,8,512]{2,1,0:T(8,128)(2,1)S(1)} %broadcast_in_dim.27, s32[128]{0:T(128)S(1)} %get-tuple-element.54, bf16[128,512]{1,0:T(8,128)(2,1)S(1)} %fusion.3), kind=kCustom, calls=%fused_computation.2 | custom fusion | bytes 394240 | tf_op jit(solution)/shard_map/scatter | solution.py:33
  17.0 48.5 %all_to_all.26 = bf16[64,8,512]{2,1,0:T(8,128)(2,1)} all-to-all(bf16[64,8,512]{2,1,0:T(8,128)(2,1)S(1)} %scatter_fusion.1), channel_id=1, replica_groups=mesh['clu'=64,'grp'=8] {'clu'}, dimensions={0} | all-to-all | bytes 1048576 | tf_op jit(solution)/shard_map/all_to_all | solution.py:36
  65.5 0.0 all-gather.3.cloned.1.call-update
  65.5 0.0 copy-done
  65.6 6.4 %scatter_fusion = s32[64,8]{0,1:T(8,128)S(1)} fusion(s32[64,8]{0,1:T(8,128)S(1)} %broadcast_in_dim.24, s32[128]{0:T(128)S(1)} %get-tuple-element.54, s32[128]{0:T(128)S(1)} %copy-done), kind=kCustom, calls=%fused_computation.1 | custom fusion | bytes 2560 | tf_op jit(solution)/shard_map/scatter | solution.py:34
  72.0 0.7 copy.9
  72.7 8.5 %all-to-all-start = ((s32[64,1,8]{2,1,0:T(1,128)}), s32[64,1,8]{2,1,0:T(1,128)S(1)}, u32[]{:S(2)}, u32[]{:S(2)}) async-start(s32[64,1,8]{2,1,0:T(1,128)} %copy.9), calls=%async_computation | async-start | bytes 65536 | tf_op jit(solution)/shard_map/all_to_all | solution.py:37
  81.2 13.1 %all-to-all-done = s32[64,1,8]{2,1,0:T(1,128)S(1)} async-done(((s32[64,1,8]{2,1,0:T(1,128)}), s32[64,1,8]{2,1,0:T(1,128)S(1)}, u32[]{:S(2)}, u32[]{:S(2)}) %all-to-all-start) | async-done | bytes 2080 | tf_op jit(solution)/shard_map/all_to_all | solution.py:37
  94.4 0.5 broadcast.179
  94.9 0.6 reduce.3
  95.5 0.1 reshape.83
  95.6 14.8 %all-gather = s32[8,1,512]{2,1,0:T(1,128)S(1)} all-gather(s32[1,1,512]{2,1,0:T(1,128)S(1)} %reshape.83), channel_id=1, replica_groups=mesh['clu'=64,'grp'=8] {'grp'}, dimensions={0}, use_global_device_ids=true | all-gather | bytes 18432 | tf_op jit(solution)/shard_map/all_gather | solution.py:45
  110.4 0.0 all-gather.3.cloned.1.call-done
  110.4 5.8 %conditional.1 = (f32[512]{0:T(512)S(1)}) conditional(s32[]{:T(128)} %convert_element_type.12, () %tuple.11, (s32[4096]{0:T(1024)S(1)}, s32[4096]{0:T(1024)S(1)}, s32[]{:T(128)}, s32[512]{0:T(512)S(1)}, s32[64,1,8]{2,1,0:T(1,128)S(1)}, /*index=5*/bf16[512,512]{1,0:T(8,128)(2,1)}, bf16[4096,512]{1,0:T(8,128)(2,1)}) %tuple.22), branch_computations={%region_6.7_spmd, %region_7.9_spmd} | conditional | flops 2162168320 | bytes 4794380 | solution.py:52
  110.4 0.1 eq.0
  110.5 5.7 %fusion.1 = f32[512]{0:T(512)S(1)} fusion(s32[4096]{0:T(1024)S(1)} %get-tuple-element.25, s32[4096]{0:T(1024)S(1)} %get-tuple-element.26, s32[512]{0:T(512)S(1)} %eq.0, s32[512]{0:T(512)S(1)} %broadcast_add_fusion, pred[4096]{0:T(1024)(128)(4,1)S(1)} %broadcast_compare_fusion, bf16[512,512]{1,0:T(8,128)(2,1)} %get-tuple-element.30, ...), kind=kOutput, calls=%fused_computation.5 | convolution fusion | flops 2162163200 | bytes 4761600 | tf_op jit(solution)/shard_map/cond/branch_1_fun/dot_general | solution.py:14
  116.2 0.1 all_to_all.20
  116.3 19.3 %all_to_all.27 = f32[64,1,8]{2,1,0:T(1,128)S(1)} all-to-all(f32[64,1,8]{2,1,0:T(1,128)S(1)} %bitcast.51), channel_id=1, replica_groups=mesh['clu'=64,'grp'=8] {'clu'}, dimensions={0} | all-to-all | bytes 4096 | tf_op jit(solution)/shard_map/all_to_all | solution.py:53
  135.6 1.8 %gather_fusion = f32[128]{0:T(128)} fusion(f32[64,8]{1,0:T(8,128)S(1)} %bitcast.47, s32[128]{0:T(128)S(1)} %get-tuple-element.53), kind=kCustom, calls=%fused_computation | custom fusion | bytes 2048 | tf_op jit(solution)/shard_map/gather | solution.py:56
  (9 shorter events, 0.1 us)
Async XLA Ops:
  6.5 59.0 %copy-start = (s32[128]{0:T(128)S(1)}, s32[128]{0:T(128)}, u32[]{:S(2)}) copy-start(s32[128]{0:T(128)} %param.6) | copy-start | bytes 1540
  6.5 103.8 %all-gather.3.cloned.1.call-start = ((), (), s32[]{:S(2)}) async-start(), calls=%async_computation.3 | async-start | bytes 4718592 | tf_op jit(solution)/shard_map/all_gather | solution.py:44
  72.7 21.7 %all-to-all-start = ((s32[64,1,8]{2,1,0:T(1,128)}), s32[64,1,8]{2,1,0:T(1,128)S(1)}, u32[]{:S(2)}, u32[]{:S(2)}) async-start(s32[64,1,8]{2,1,0:T(1,128)} %copy.9), calls=%async_computation | async-start | bytes 65536 | tf_op jit(solution)/shard_map/all_to_all | solution.py:37
Sparse Core Ops, SparseCore 0:
  65.7 35.3 all-gather.2
where the time goes:
time: 145 us; the launch traced here: 144 us
  blocking collectives  82.6 us (57%)
  local copies, waits for them, and re-layouts  16.8 us (12%)
  between operations  13.5 us (9%)
  waiting for transfers between devices  13.2 us (9%)
  starting transfers between devices  8.53 us (6%)
  matrix products  5.7 us (4%)
  other arithmetic  3.97 us (3%)
    all_to_all x1, blocking collectives, shards(): lax.all_to_all(send_units, 'clu', split_axis=0, concat_axis=0, tiled=True)  48.5 us
    all_to_all x1, blocking collectives, shards(): lax.all_to_all(best.reshape(n_clu, slots), 'clu', split_axis=0, concat_ax...  19.3 us
    all_gather x1, blocking collectives, shards(): key_cl = lax.all_gather(query_cl, 'grp', axis=0, tiled=True)  14.8 us
    all_to_all x1, waiting for transfers between devices, shards(): lax.all_to_all(send_clusters, 'clu', split_axis=0, concat_axis=0, tiled=T...  13.1 us
    all_to_all x1, starting transfers between devices, shards(): lax.all_to_all(send_clusters, 'clu', split_axis=0, concat_axis=0, tiled=T...  8.53 us
    scatter x1, local copies, waits for them, and re-layouts, shards(): jnp.zeros((n_clu, slots, width), jnp.bfloat16).at[dest, position].set(unit)  7.05 us
    scatter x1, local copies, waits for them, and re-layouts, shards(): jnp.full((n_clu, slots), -1, jnp.int32).at[dest, position].set(cluster_id)  6.43 us
    dot_general x1, matrix products, tile_max(): lax.dot_general(queries, keys, (((1,), (1,)), ((), ())), preferred_elemen...  5.7 us
  transfers between devices with their start and end apart: 2, of which 1 were waited for; matrix products, arithmetic and copies ran while one was open for 6% of the time, Pallas kernels for 0%

commit v1 on v0

v1 whole, which is shorter than its diff:
```python
import functools

import jax
import jax.numpy as jnp
from jax import lax
from jax.experimental import pallas as pl
from jax.experimental.pallas import tpu as pltpu
from jax.sharding import PartitionSpec as P

MESH = pl.DeviceIdType.MESH
NX, NY, NZ, NC = 4, 4, 16, 2
R, D = 128, 512
NEAR = 4
NEAR_SLOTS = 2 * NEAR + 1
FAR_SLOTS = NZ - NEAR_SLOTS
PLANE = NX * NY * NC
TILE = 4 * R
NT = (((1,), (1,)), ((), ()))


def kernel(
    emb_ref, cid_ref, table_ref, out_ref,
    kb, qb, km, qm, qcl, qgr, kcl, kgr, acc_near, acc_far,
    near_out, near_in, far_out, far_in,
    zs, zr, zms, zmr, qs, qr, qms, qmr, ds, dr, dms, dmr, ns, nr, fs, fr,
):
    clu, grp = lax.axis_index("clu"), lax.axis_index("grp")
    x, z = clu // NZ, clu % NZ
    y, c = grp // NC, grp % NC
    row = y * NC + c
    me = row * NX + x

    def dev(dx=0, dy=0, dz=0, flip=False):
        xx, yy, zz = (x + dx) % NX, (y + dy) % NY, (z + dz) % NZ
        cc = 1 - c if flip else c
        return (xx * NZ + zz, yy * NC + cc)

    def slot(dx, dy, flip=False):
        cc = 1 - c if flip else c
        return (((y + dy) % NY) * NC + cc) * NX + (x + dx) % NX

    barrier = pltpu.get_barrier_semaphore()
    for step in (dict(dx=1), dict(dx=-1), dict(dy=1), dict(dy=-1), dict(dz=1), dict(dz=-1), dict(flip=True)):
        pl.semaphore_signal(barrier, inc=1, device_id=dev(**step), device_id_type=MESH)

    values = emb_ref[...].astype(jnp.float32)
    scale = lax.rsqrt(jnp.sum(values * values, axis=1, keepdims=True) + 1e-06)
    unit = (values * scale).astype(jnp.bfloat16)
    kb[0] = unit
    qb[me] = unit
    eye = lax.broadcasted_iota(jnp.int32, (R, R), 0) == lax.broadcasted_iota(jnp.int32, (R, R), 1)
    sub = lax.broadcasted_iota(jnp.int32, (R, R), 0)
    ones = jnp.ones((R, R), jnp.bfloat16)

    def column(line):
        spread = jnp.where(eye, jnp.broadcast_to(line, (R, R)), 0.0).astype(jnp.bfloat16)
        return jnp.dot(spread, ones, preferred_element_type=jnp.float32)

    cid = cid_ref[...]
    group = jnp.zeros((1, R), jnp.float32)
    for h in range(2):
        part = column(table_ref[:, h * R:(h + 1) * R].astype(jnp.float32))
        group += jnp.sum(jnp.where(jnp.broadcast_to(cid, (R, R)) == sub + h * R, part, 0.0), axis=0, keepdims=True)
    cluster = cid.astype(jnp.float32)
    km[0, 0:1, :] = cluster
    km[0, 1:2, :] = group
    qm[me, 0:1, :] = cluster
    qm[me, 1:2, :] = group

    pending = []

    def rc(src, dst, s, r, where):
        return pltpu.make_async_remote_copy(
            src_ref=src, dst_ref=dst, send_sem=s, recv_sem=r, device_id=where, device_id_type=MESH)

    def go(copy):
        copy.start()
        pending.append(copy)

    half = R // 2

    def ring(d, sign, part):
        lo = part * half
        if sign > 0:
            src = 0 if d == 1 else 2 * d - 3
            dst = 2 * d - 1
        else:
            src = 0 if d == 1 else 2 * d - 2
            dst = 2 * d if d < 8 else 15
        i = (d - 1) * 4 + (0 if sign > 0 else 2) + part
        rows = pl.ds(lo, half)
        return rc(kb.at[src, rows], kb.at[dst, rows], zs.at[i], zr.at[i], dev(dz=sign))

    def ring_meta(d, sign):
        if sign > 0:
            src, dst = (0 if d == 1 else 2 * d - 3), 2 * d - 1
        else:
            src, dst = (0 if d == 1 else 2 * d - 2), 2 * d
        i = (d - 1) * 2 + (0 if sign > 0 else 1)
        return rc(km.at[src], km.at[dst], zms.at[i], zmr.at[i], dev(dz=sign))

    def has(d, sign, part):
        return d < 8 or (sign > 0) == (part == 0)

    def has_meta(d, sign):
        return d < 8 or sign > 0

    def send(d, part):
        for sign in (1, -1):
            if has(d, sign, part):
                go(ring(d, sign, part))

    def send_meta(d):
        for sign in (1, -1):
            if has_meta(d, sign):
                go(ring_meta(d, sign))

    def pump(d, part):
        for sign in (1, -1):
            if has(d, sign, part):
                ring(d, sign, part).wait_recv()
                if d < 8 and has(d + 1, sign, part):
                    go(ring(d + 1, sign, part))
        if part == 0:
            for sign in (1, -1):
                if has_meta(d, sign):
                    ring_meta(d, sign).wait_recv()
                    if d < 8 and has_meta(d + 1, sign):
                        go(ring_meta(d + 1, sign))

    def move(h, phase, other, kind):
        along_x = (h == 0) == (phase == 0)
        step = 1 if kind[-1] == "+" else -1
        lo, n = h * half, half
        off = 0
        if kind[0] == "f":
            n = half // 2
            lo += 0 if step > 0 else n
            off = -step
        if along_x:
            s = slot(off, other if phase == 1 else 0)
            target = dev(dx=step)
        else:
            s = slot(other if phase == 1 else 0, off)
            target = dev(dy=step)
        i = h * 20 + (0 if phase == 0 else 4 + 4 * (other % 4)) + ("+", "-", "f+", "f-").index(kind)
        ref = qb.at[s, pl.ds(lo, n)]
        return rc(ref, ref, qs.at[i], qr.at[i], target)

    def move_meta(phase, other, kind):
        step = -1 if kind == "-" else 1
        off = -1 if kind == "f+" else 0
        if phase == 0:
            s, target = slot(off, 0), dev(dx=step)
        else:
            s, target = slot(other, off), dev(dy=step)
        i = (0 if phase == 0 else 3 + 3 * (other % 4)) + ("+", "-", "f+").index(kind)
        return rc(qm.at[s], qm.at[s], qms.at[i], qmr.at[i], target)

    def share(dx, dy):
        s = slot(dx, dy)
        i = (dy % 4) * 4 + dx % 4
        return (rc(qb.at[s], qb.at[s], ds.at[i], dr.at[i], dev(flip=True)),
                rc(qm.at[s], qm.at[s], dms.at[i], dmr.at[i], dev(flip=True)))

    def give(dx, dy):
        for copy in share(dx, dy):
            go(copy)

    pl.semaphore_wait(barrier, 7)

    send_meta(1)
    go(move_meta(0, 0, "+"))
    go(move_meta(0, 0, "-"))
    go(move_meta(1, 0, "+"))
    go(move_meta(1, 0, "-"))
    send(1, 0)
    for h in range(2):
        go(move(h, 0, 0, "+"))
        go(move(h, 0, 0, "-"))
    send(1, 1)
    for h in range(2):
        go(move(h, 1, 0, "+"))
        go(move(h, 1, 0, "-"))
    give(0, 0)
    for sign, off in (("+", -1), ("-", 1)):
        for h in range(2):
            move(h, 0, 0, sign).wait_recv()
            go(move(h, 0, 0, "f" + sign))
        move_meta(0, 0, sign).wait_recv()
        if sign == "+":
            go(move_meta(0, 0, "f+"))
        go(move_meta(1, off, "+"))
        go(move_meta(1, off, "-"))
        for h in range(2):
            go(move(h, 1, off, "+"))
            go(move(h, 1, off, "-"))
    pump(1, 0)
    pump(1, 1)
    for sign in ("+", "-"):
        for h in range(2):
            move(h, 1, 0, sign).wait_recv()
            go(move(h, 1, 0, "f" + sign))
        move_meta(1, 0, sign).wait_recv()
        if sign == "+":
            go(move_meta(1, 0, "f+"))
    give(-1, 0)
    give(1, 0)
    give(0, -1)
    give(0, 1)
    for h in range(2):
        for sign in ("+", "-"):
            move(h, 0, 0, "f" + sign).wait_recv()
    move_meta(0, 0, "f+").wait_recv()
    go(move_meta(1, 2, "+"))
    go(move_meta(1, 2, "-"))
    for h in range(2):
        go(move(h, 1, 2, "+"))
        go(move(h, 1, 2, "-"))
    pump(2, 0)
    pump(2, 1)
    for off in (-1, 1):
        for sign in ("+", "-"):
            for h in range(2):
                move(h, 1, off, sign).wait_recv()
                go(move(h, 1, off, "f" + sign))
            move_meta(1, off, sign).wait_recv()
        go(move_meta(1, off, "f+"))
    for h in range(2):
        for sign in ("+", "-"):
            move(h, 1, 0, "f" + sign).wait_recv()
    move_meta(1, 0, "f+").wait_recv()
    for dx, dy in ((-1, -1), (-1, 1), (1, -1), (1, 1), (2, 0), (0, 2)):
        give(dx, dy)
    pump(3, 0)
    pump(3, 1)
    for sign in ("+", "-"):
        for h in range(2):
            move(h, 1, 2, sign).wait_recv()
            go(move(h, 1, 2, "f" + sign))
        move_meta(1, 2, sign).wait_recv()
    go(move_meta(1, 2, "f+"))
    for off in (-1, 1):
        for h in range(2):
            for sign in ("+", "-"):
                move(h, 1, off, "f" + sign).wait_recv()
        move_meta(1, off, "f+").wait_recv()
    for dx, dy in ((2, -1), (2, 1), (-1, 2), (1, 2)):
        give(dx, dy)
    for h in range(2):
        for sign in ("+", "-"):
            move(h, 1, 2, "f" + sign).wait_recv()
    move_meta(1, 2, "f+").wait_recv()
    give(2, 2)
    pump(4, 0)
    for dy in range(NY):
        for dx in range(NX):
            for copy in share(dx, dy):
                copy.wait_recv()

    acc_near[...] = jnp.full(acc_near.shape, -1.0, jnp.float32)
    acc_far[...] = jnp.full(acc_far.shape, -1.0, jnp.float32)

    def q_columns(s, carry):
        rows = pl.ds(pl.multiple_of(s * R, R), R)
        qcl[rows, :] = column(qm[s, 0:1, :])
        qgr[rows, :] = jnp.where(s < me, column(qm[s, 1:2, :]), -1.0)
        return carry

    lax.fori_loop(0, PLANE, q_columns, 0)

    def tile(stream, lanes, s_cl, s_gr, l_cl, l_gr, acc, at):
        sims = lax.dot_general(stream, lanes, NT, preferred_element_type=jnp.float32)
        n = sims.shape[0] // 8
        for j in range(sims.shape[1] // R):
            s = sims[:, j * R:(j + 1) * R]
            score = jnp.where(s_cl == l_cl[j], s, 0.5 * s)
            gr = s_gr[j] if isinstance(s_gr, list) else s_gr
            score = jnp.where(gr == l_gr[j], score, -1.0)
            best = jnp.max(score.reshape(n, 8, R), axis=0)
            where = pl.ds(pl.multiple_of(at + j * R, R), R)
            acc[:, where] = jnp.maximum(acc[:, where], best)

    def lines(ref, s, n, ok=None):
        cl = [ref[s + j, 0:1, :] for j in range(n)]
        gr = [ref[s + j, 1:2, :] for j in range(n)]
        return cl, gr

    def near(t, first, n):
        rows = pl.ds(pl.multiple_of(t * TILE, TILE), TILE)
        stream = qb[pl.ds(t * 4, 4)].reshape(TILE, D)
        cl, gr = lines(km, first, n)
        lanes = kb[first:first + n].reshape(n * R, D)
        tile(stream, lanes, qcl[rows, :], qgr[rows, :], cl, gr, acc_near, first * R)

    def k_columns(s):
        rows = pl.ds((s - NEAR_SLOTS) * R, R)
        kcl[rows, :] = column(km[s, 0:1, :])
        kgr[rows, :] = column(km[s, 1:2, :])

    def far(t, first, n, wide):
        rows = pl.ds((first - NEAR_SLOTS) * R, n * R)
        stream = kb[first:first + n].reshape(n * R, D)
        lanes = qb[pl.ds(t * 4, wide)].reshape(wide * R, D)
        cl, gr = lines(qm, t * 4, wide)
        gr = [jnp.where(t * 4 + j > me, g, -2.0) for j, g in enumerate(gr)]
        tile(stream, lanes, kcl[rows, :], kgr[rows, :], cl, gr, acc_far, t * TILE)

    def origin(s):
        if s == 0:
            return z
        d = (s + 1) // 2
        return (z - d) % NZ if s % 2 else (z + d) % NZ

    def own_near():
        stream = kb[0]
        cl, gr = lines(km, 0, NEAR_SLOTS)
        s_cl, s_gr = column(cl[0]), column(gr[0])
        lane = lax.broadcasted_iota(jnp.int32, (R, R), 1)
        groups = [jnp.where(sub < lane, s_gr, -1.0)]
        for s in range(1, NEAR_SLOTS):
            groups.append(jnp.where(origin(s) > z, s_gr, -1.0))
        tile(stream, kb[0:NEAR_SLOTS].reshape(NEAR_SLOTS * R, D), s_cl, groups, cl, gr, acc_near, 0)

    def own_far(first, n):
        stream = kb[first:first + n].reshape(n * R, D)
        rows = pl.ds((first - NEAR_SLOTS) * R, n * R)
        groups = jnp.concatenate(
            [jnp.where(origin(first + j) < z, kgr[pl.ds((first + j - NEAR_SLOTS) * R, R), :], -1.0) for j in range(n)], axis=0)
        tile(stream, kb[0], kcl[rows, :], groups, [km[0, 0:1, :]], [km[0, 1:2, :]], acc_far, me * R)

    def near_if(t):
        @pl.when(t * 4 < me)
        def _():
            near(t, 0, NEAR_SLOTS)

    def far_loop(first, n):
        def body(t, carry):
            far(t, first, n, 4)
            return carry
        lax.fori_loop((me + 1) // 4, PLANE // 4, body, 0)

    pump(4, 1)
    own_near()
    near_if(0)
    pump(5, 0)
    near_if(1)
    pump(5, 1)
    near_if(2)
    near_if(3)
    pump(6, 0)
    k_columns(9)
    k_columns(10)
    far_loop(9, 2)
    near_if(4)
    pump(6, 1)
    near_if(5)
    pump(7, 0)
    k_columns(11)
    k_columns(12)
    far_loop(11, 2)
    near_if(6)
    pump(7, 1)
    near_if(7)

    def back(s):
        d = (s + 1) // 2
        step, other = (-d, 2 * d) if s % 2 else (d, 2 * d - 1)
        return rc(near_out.at[s], near_in.at[other], ns.at[s], nr.at[s], dev(dz=step))

    for s in range(NEAR_SLOTS):
        near_out[s] = jnp.max(acc_near[:, s * R:(s + 1) * R], axis=0, keepdims=True)
    for s in range(1, NEAR_SLOTS):
        go(back(s))
    k_columns(13)
    k_columns(14)
    far_loop(13, 2)
    pump(8, 0)
    pump(8, 1)
    k_columns(15)
    far_loop(15, 1)
    own_far(NEAR_SLOTS, FAR_SLOTS)

    for s in range(PLANE):
        far_out[s] = jnp.max(acc_far[:, s * R:(s + 1) * R], axis=0, keepdims=True)

    def reply(k):
        dx, dy, flip = k % NX, (k // NX) % NY, k >= NX * NY
        return rc(far_out.at[slot(dx, dy, flip)], far_in.at[k], fs.at[k], fr.at[k], dev(dx, dy, 0, flip))

    for k in range(1, PLANE):
        go(reply(k))
    best = jnp.maximum(near_out[0], far_out[me])
    for s in range(1, NEAR_SLOTS):
        back(s).wait_recv()
    for s in range(1, NEAR_SLOTS):
        best = jnp.maximum(best, near_in[s])
    for k in range(1, PLANE):
        reply(k).wait_recv()
    for k in range(1, PLANE):
        best = jnp.maximum(best, far_in[k])
    out_ref[...] = best
    for copy in pending:
        copy.wait_send()


def solution(mesh):
    def step(embeddings, cluster_id, cluster_group):
        dma = pltpu.SemaphoreType.DMA
        f32 = jnp.float32
        best = pl.pallas_call(
            kernel,
            out_shape=jax.ShapeDtypeStruct((1, R), f32),
            in_specs=[pl.BlockSpec(memory_space=pltpu.VMEM)] * 3,
            out_specs=pl.BlockSpec(memory_space=pltpu.VMEM),
            scratch_shapes=[
                pltpu.VMEM((NZ, R, D), jnp.bfloat16),
                pltpu.VMEM((PLANE, R, D), jnp.bfloat16),
                pltpu.VMEM((NZ, 2, R), f32),
                pltpu.VMEM((PLANE, 2, R), f32),
                pltpu.VMEM((PLANE * R, R), f32),
                pltpu.VMEM((PLANE * R, R), f32),
                pltpu.VMEM((FAR_SLOTS * R, R), f32),
                pltpu.VMEM((FAR_SLOTS * R, R), f32),
                pltpu.VMEM((8, NEAR_SLOTS * R), f32),
                pltpu.VMEM((8, PLANE * R), f32),
                pltpu.VMEM((NEAR_SLOTS, 1, R), f32),
                pltpu.VMEM((NEAR_SLOTS, 1, R), f32),
                pltpu.VMEM((PLANE, 1, R), f32),
                pltpu.VMEM((PLANE, 1, R), f32),
                dma((32,)), dma((32,)), dma((16,)), dma((16,)),
                dma((40,)), dma((40,)), dma((15,)), dma((15,)),
                dma((16,)), dma((16,)), dma((16,)), dma((16,)),
                dma((NEAR_SLOTS,)), dma((NEAR_SLOTS,)), dma((PLANE,)), dma((PLANE,)),
            ],
            compiler_params=pltpu.CompilerParams(
                collective_id=0, has_side_effects=True, vmem_limit_bytes=60 * 2**20),
        )(embeddings, cluster_id.reshape(1, R), cluster_group.reshape(1, -1))
        return best.reshape(R)

    placed = (P(("clu", "grp"), None), P(("clu", "grp")), P())
    return jax.shard_map(step, mesh=mesh, in_specs=placed, out_specs=P(("clu", "grp")), check_vma=False)
```

time: 145 us -> 66.2 us (0.46)
  blocking collectives: 82.6 us -> 0 us
  Pallas kernels: 0 us -> 65 us
  local copies, waits for them, and re-layouts: 16.8 us -> 1.1 us
  between operations: 13.5 us -> 0.02 us
  waiting for transfers between devices: 13.2 us -> 0 us
  starting transfers between devices: 8.53 us -> 0 us
  matrix products: 5.7 us -> 0 us
  other arithmetic: 3.97 us -> 0 us
    all_to_all x2 -> x0, blocking collectives: 67.8 us -> none  [the longest x1 48.5 us: shards(): lax.all_to_all(send_units, 'clu', split_axis=0, concat_axis=0, tiled=True)]
    pallas_call x0 -> x1, Pallas kernels: none -> 65 us  [step(): pl.pallas_call(kernel, out_shape=jax.ShapeDtypeStruct((1, R), f32), in_sp...]
    all_gather x1 -> x0, blocking collectives: 14.8 us -> none  [shards(): key_cl = lax.all_gather(query_cl, 'grp', axis=0, tiled=True)]
    scatter x2 -> x0, local copies, waits for them, and re-layouts: 13.5 us -> none  [the longest x1 7.05 us: shards(): jnp.zeros((n_clu, slots, width), jnp.bfloat16).at[dest, position].set(unit)]
    all_to_all x1 -> x0, waiting for transfers between devices: 13.1 us -> none  [shards(): lax.all_to_all(send_clusters, 'clu', split_axis=0, concat_axis=0, tiled=T...]
    all_to_all x1 -> x0, starting transfers between devices: 8.53 us -> none  [shards(): lax.all_to_all(send_clusters, 'clu', split_axis=0, concat_axis=0, tiled=T...]
    dot_general x1 -> x0, matrix products: 5.7 us -> none  [tile_max(): lax.dot_general(queries, keys, (((1,), (1,)), ((), ())), preferred_elemen...]
    reduce_sum x3 -> x0, other arithmetic: 2.05 us -> none  [the longest x1 1.02 us: normalize(): scale = lax.rsqrt(jnp.sum(values * values, axis=-1, keepdims=True) + 1e-06)]
  transfers between devices with their start and end apart: 2 -> 0, of which waited for: 1 -> 0; matrix products, arithmetic and copies ran while one was open for 6% -> 0% of each run, Pallas kernels for 0% -> 0%
where the time goes in v1:
time: 66.2 us; the launch traced here: 66.1 us
  Pallas kernels  65 us (98%)
  local copies, waits for them, and re-layouts  1.1 us (2%)
    pallas_call x1, Pallas kernels, step(): pl.pallas_call(kernel, out_shape=jax.ShapeDtypeStruct((1, R), f32), in_sp...  65 us

profile of v1, /device:TPU:1, one launch (start us, length us, event | category | flops | bytes accessed | tf_op | source)
XLA Modules:
  0.0 66.1 jit_solution(3471539984498981450)
XLA Ops:
  0.0 65.0 %shard_map.37 = f32[1,128]{1,0:T(1,128)} custom-call(bf16[128,512]{1,0:T(8,128)(2,1)} %emb_ref.1, s32[1,128]{1,0:T(1,128)} %bitcast.4, s32[1,256]{1,0:T(1,128)} %bitcast.3), custom_call_target="tpu_custom_call" | custom-call | tf_op jit(solution)/shard_map/pallas_call | solution.py:411
  65.0 0.0 copy-start
  65.0 0.6 copy-done
  65.6 0.5 copy.5
Async XLA Ops:
  65.0 0.6 copy-start

commit v2 on v1

--- a/solution.py
+++ b/solution.py
@@ -12,7 +12,6 @@
 R, D = 128, 512
 NEAR = 4
 NEAR_SLOTS = 2 * NEAR + 1
-FAR_SLOTS = NZ - NEAR_SLOTS
 PLANE = NX * NY * NC
 TILE = 4 * R
 NT = (((1,), (1,)), ((), ()))
@@ -20,7 +19,7 @@
 
 def kernel(
     emb_ref, cid_ref, table_ref, out_ref,
-    kb, qb, km, qm, qcl, qgr, kcl, kgr, acc_near, acc_far,
+    kb, qb, km, qm, kcl, kgr, acc_near, acc_far,
     near_out, near_in, far_out, far_in,
     zs, zr, zms, zmr, qs, qr, qms, qmr, ds, dr, dms, dmr, ns, nr, fs, fr,
 ):
@@ -31,13 +30,13 @@
     me = row * NX + x
 
     def dev(dx=0, dy=0, dz=0, flip=False):
-        xx, yy, zz = (x + dx) % NX, (y + dy) % NY, (z + dz) % NZ
+        xx, yy, zz = (x + dx) & 3, (y + dy) & 3, (z + dz) & 15
         cc = 1 - c if flip else c
         return (xx * NZ + zz, yy * NC + cc)
 
     def slot(dx, dy, flip=False):
         cc = 1 - c if flip else c
-        return (((y + dy) % NY) * NC + cc) * NX + (x + dx) % NX
+        return (((y + dy) & 3) * NC + cc) * NX + ((x + dx) & 3)
 
     barrier = pltpu.get_barrier_semaphore()
     for step in (dict(dx=1), dict(dx=-1), dict(dy=1), dict(dy=-1), dict(dz=1), dict(dz=-1), dict(flip=True)):
@@ -79,16 +78,13 @@
 
     half = R // 2
 
-    def ring(d, sign, part):
-        lo = part * half
+    def ring(d, sign):
         if sign > 0:
-            src = 0 if d == 1 else 2 * d - 3
-            dst = 2 * d - 1
+            src, dst, lo = (0 if d == 1 else 2 * d - 3), 2 * d - 1, 0
         else:
-            src = 0 if d == 1 else 2 * d - 2
-            dst = 2 * d if d < 8 else 15
-        i = (d - 1) * 4 + (0 if sign > 0 else 2) + part
-        rows = pl.ds(lo, half)
+            src, dst, lo = (0 if d == 1 else 2 * d - 2), min(2 * d, 15), half
+        i = (d - 1) * 2 + (0 if sign > 0 else 1)
+        rows = pl.ds(lo, half) if d == 8 else pl.ds(0, R)
         return rc(kb.at[src, rows], kb.at[dst, rows], zs.at[i], zr.at[i], dev(dz=sign))
 
     def ring_meta(d, sign):
@@ -99,34 +95,21 @@
         i = (d - 1) * 2 + (0 if sign > 0 else 1)
         return rc(km.at[src], km.at[dst], zms.at[i], zmr.at[i], dev(dz=sign))
 
-    def has(d, sign, part):
-        return d < 8 or (sign > 0) == (part == 0)
-
-    def has_meta(d, sign):
-        return d < 8 or sign > 0
-
-    def send(d, part):
+    def forward(d):
         for sign in (1, -1):
-            if has(d, sign, part):
-                go(ring(d, sign, part))
-
-    def send_meta(d):
+            go(ring(d, sign))
+        for sign in (1, -1) if d < 8 else (1,):
+            go(ring_meta(d, sign))
+
+    def pump(d):
         for sign in (1, -1):
-            if has_meta(d, sign):
-                go(ring_meta(d, sign))
-
-    def pump(d, part):
-        for sign in (1, -1):
-            if has(d, sign, part):
-                ring(d, sign, part).wait_recv()
-                if d < 8 and has(d + 1, sign, part):
-                    go(ring(d + 1, sign, part))
-        if part == 0:
-            for sign in (1, -1):
-                if has_meta(d, sign):
-                    ring_meta(d, sign).wait_recv()
-                    if d < 8 and has_meta(d + 1, sign):
-                        go(ring_meta(d + 1, sign))
+            ring(d, sign).wait_recv()
+            if d < 8:
+                go(ring(d + 1, sign))
+        for sign in (1, -1) if d < 8 else (1,):
+            ring_meta(d, sign).wait_recv()
+            if d < 7 or (d == 7 and sign > 0):
+                go(ring_meta(d + 1, sign))
 
     def move(h, phase, other, kind):
         along_x = (h == 0) == (phase == 0)
@@ -169,16 +152,14 @@
 
     pl.semaphore_wait(barrier, 7)
 
-    send_meta(1)
+    forward(1)
     go(move_meta(0, 0, "+"))
     go(move_meta(0, 0, "-"))
     go(move_meta(1, 0, "+"))
     go(move_meta(1, 0, "-"))
-    send(1, 0)
     for h in range(2):
         go(move(h, 0, 0, "+"))
         go(move(h, 0, 0, "-"))
-    send(1, 1)
     for h in range(2):
         go(move(h, 1, 0, "+"))
         go(move(h, 1, 0, "-"))
@@ -195,8 +176,7 @@
         for h in range(2):
             go(move(h, 1, off, "+"))
             go(move(h, 1, off, "-"))
-    pump(1, 0)
-    pump(1, 1)
+    pump(1)
     for sign in ("+", "-"):
         for h in range(2):
             move(h, 1, 0, sign).wait_recv()
@@ -217,8 +197,7 @@
     for h in range(2):
         go(move(h, 1, 2, "+"))
         go(move(h, 1, 2, "-"))
-    pump(2, 0)
-    pump(2, 1)
+    pump(2)
     for off in (-1, 1):
         for sign in ("+", "-"):
             for h in range(2):
@@ -232,8 +211,7 @@
     move_meta(1, 0, "f+").wait_recv()
     for dx, dy in ((-1, -1), (-1, 1), (1, -1), (1, 1), (2, 0), (0, 2)):
         give(dx, dy)
-    pump(3, 0)
-    pump(3, 1)
+    pump(3)
     for sign in ("+", "-"):
         for h in range(2):
             move(h, 1, 2, sign).wait_recv()
@@ -252,116 +230,111 @@
             move(h, 1, 2, "f" + sign).wait_recv()
     move_meta(1, 2, "f+").wait_recv()
     give(2, 2)
-    pump(4, 0)
+    pump(4)
+    acc_near[...] = jnp.full(acc_near.shape, -1.0, jnp.float32)
+    acc_far[...] = jnp.full(acc_far.shape, -1.0, jnp.float32)
+
+    def k_columns(first, n):
+        for s in range(first, first + n):
+            rows = pl.ds(s * R, R)
+            kcl[rows, :] = column(km[s, 0:1, :])
+            kgr[rows, :] = column(km[s, 1:2, :])
+
+    def scores(sims, j, s_cl, s_gr, l_cl, l_gr):
+        s = sims[:, j * R:(j + 1) * R]
+        score = jnp.where(s_cl == l_cl, s, 0.5 * s)
+        return jnp.where(s_gr == l_gr, score, -1.0)
+
+    def near(t):
+        stream = kb[0:NEAR_SLOTS].reshape(NEAR_SLOTS * R, D)
+        lanes = qb[pl.ds(t * 4, 4)].reshape(TILE, D)
+        sims = lax.dot_general(stream, lanes, NT, preferred_element_type=jnp.float32)
+        rows = pl.ds(0, NEAR_SLOTS * R)
+        best = acc_near[...]
+        for j in range(4):
+            q = t * 4 + j
+            gr = jnp.where(q < me, qm[q, 1:2, :], -2.0)
+            best = jnp.maximum(best, scores(sims, j, kcl[rows, :], kgr[rows, :], qm[q, 0:1, :], gr))
+        acc_near[...] = best
+
+    def near_loop(lo, hi):
+        def body(t, carry):
+            near(t)
+            return carry
+        lax.fori_loop(lo, hi, body, 0)
+
+    def origin(s):
+        if s == 0:
+            return z
+        d = (s + 1) // 2
+        return (z - d) & 15 if s % 2 else (z + d) & 15
+
+    def own_near():
+        stream = kb[0:NEAR_SLOTS].reshape(NEAR_SLOTS * R, D)
+        sims = lax.dot_general(stream, kb[0], NT, preferred_element_type=jnp.float32)
+        rows = pl.ds(0, NEAR_SLOTS * R)
+        lane = lax.broadcasted_iota(jnp.int32, (R, R), 1)
+        groups = [jnp.where(sub > lane, kgr[0:R, :], -1.0)]
+        for s in range(1, NEAR_SLOTS):
+            groups.append(jnp.where(origin(s) > z, kgr[s * R:(s + 1) * R, :], -1.0))
+        acc_near[...] = jnp.maximum(acc_near[...], scores(
+            sims, 0, kcl[rows, :], jnp.concatenate(groups, axis=0), km[0, 0:1, :], km[0, 1:2, :]))
+
+    def into_far(best, s):
+        where = pl.ds(pl.multiple_of(s * R, R), R)
+        n = best.shape[0] // 8
+        acc_far[:, where] = jnp.maximum(acc_far[:, where], jnp.max(best.reshape(n, 8, R), axis=0))
+
+    def far(t, first, n):
+        rows = pl.ds(first * R, n * R)
+        stream = kb[first:first + n].reshape(n * R, D)
+        lanes = qb[pl.ds(t * 8, 8)].reshape(2 * TILE, D)
+        sims = lax.dot_general(stream, lanes, NT, preferred_element_type=jnp.float32)
+        for j in range(8):
+            q = t * 8 + j
+            later = q > me
+            if n == 1:
+                later = later | ((q == me) & (origin(first) < z))
+            gr = jnp.where(later, qm[q, 1:2, :], -2.0)
+            into_far(scores(sims, j, kcl[rows, :], kgr[rows, :], qm[q, 0:1, :], gr), q)
+
+    def far_loop(first, n):
+        def body(t, carry):
+            far(t, first, n)
+            return carry
+        lax.fori_loop(me // 8, PLANE // 8, body, 0)
+
+    def own_far(first, n):
+        stream = kb[first:first + n].reshape(n * R, D)
+        sims = lax.dot_general(stream, kb[0], NT, preferred_element_type=jnp.float32)
+        groups = jnp.concatenate(
+            [jnp.where(origin(s) < z, kgr[s * R:(s + 1) * R, :], -1.0) for s in range(first, first + n)], axis=0)
+        into_far(scores(sims, 0, kcl[pl.ds(first * R, n * R), :], groups, km[0, 0:1, :], km[0, 1:2, :]), me)
+
+    k_columns(0, NEAR_SLOTS)
+    own_near()
     for dy in range(NY):
         for dx in range(NX):
             for copy in share(dx, dy):
                 copy.wait_recv()
-
-    acc_near[...] = jnp.full(acc_near.shape, -1.0, jnp.float32)
-    acc_far[...] = jnp.full(acc_far.shape, -1.0, jnp.float32)
-
-    def q_columns(s, carry):
-        rows = pl.ds(pl.multiple_of(s * R, R), R)
-        qcl[rows, :] = column(qm[s, 0:1, :])
-        qgr[rows, :] = jnp.where(s < me, column(qm[s, 1:2, :]), -1.0)
-        return carry
-
-    lax.fori_loop(0, PLANE, q_columns, 0)
-
-    def tile(stream, lanes, s_cl, s_gr, l_cl, l_gr, acc, at):
-        sims = lax.dot_general(stream, lanes, NT, preferred_element_type=jnp.float32)
-        n = sims.shape[0] // 8
-        for j in range(sims.shape[1] // R):
-            s = sims[:, j * R:(j + 1) * R]
-            score = jnp.where(s_cl == l_cl[j], s, 0.5 * s)
-            gr = s_gr[j] if isinstance(s_gr, list) else s_gr
-            score = jnp.where(gr == l_gr[j], score, -1.0)
-            best = jnp.max(score.reshape(n, 8, R), axis=0)
-            where = pl.ds(pl.multiple_of(at + j * R, R), R)
-            acc[:, where] = jnp.maximum(acc[:, where], best)
-
-    def lines(ref, s, n, ok=None):
-        cl = [ref[s + j, 0:1, :] for j in range(n)]
-        gr = [ref[s + j, 1:2, :] for j in range(n)]
-        return cl, gr
-
-    def near(t, first, n):
-        rows = pl.ds(pl.multiple_of(t * TILE, TILE), TILE)
-        stream = qb[pl.ds(t * 4, 4)].reshape(TILE, D)
-        cl, gr = lines(km, first, n)
-        lanes = kb[first:first + n].reshape(n * R, D)
-        tile(stream, lanes, qcl[rows, :], qgr[rows, :], cl, gr, acc_near, first * R)
-
-    def k_columns(s):
-        rows = pl.ds((s - NEAR_SLOTS) * R, R)
-        kcl[rows, :] = column(km[s, 0:1, :])
-        kgr[rows, :] = column(km[s, 1:2, :])
-
-    def far(t, first, n, wide):
-        rows = pl.ds((first - NEAR_SLOTS) * R, n * R)
-        stream = kb[first:first + n].reshape(n * R, D)
-        lanes = qb[pl.ds(t * 4, wide)].reshape(wide * R, D)
-        cl, gr = lines(qm, t * 4, wide)
-        gr = [jnp.where(t * 4 + j > me, g, -2.0) for j, g in enumerate(gr)]
-        tile(stream, lanes, kcl[rows, :], kgr[rows, :], cl, gr, acc_far, t * TILE)
-
-    def origin(s):
-        if s == 0:
-            return z
-        d = (s + 1) // 2
-        return (z - d) % NZ if s % 2 else (z + d) % NZ
-
-    def own_near():
-        stream = kb[0]
-        cl, gr = lines(km, 0, NEAR_SLOTS)
-        s_cl, s_gr = column(cl[0]), column(gr[0])
-        lane = lax.broadcasted_iota(jnp.int32, (R, R), 1)
-        groups = [jnp.where(sub < lane, s_gr, -1.0)]
-        for s in range(1, NEAR_SLOTS):
-            groups.append(jnp.where(origin(s) > z, s_gr, -1.0))
-        tile(stream, kb[0:NEAR_SLOTS].reshape(NEAR_SLOTS * R, D), s_cl, groups, cl, gr, acc_near, 0)
-
-    def own_far(first, n):
-        stream = kb[first:first + n].reshape(n * R, D)
-        rows = pl.ds((first - NEAR_SLOTS) * R, n * R)
-        groups = jnp.concatenate(
-            [jnp.where(origin(first + j) < z, kgr[pl.ds((first + j - NEAR_SLOTS) * R, R), :], -1.0) for j in range(n)], axis=0)
-        tile(stream, kb[0], kcl[rows, :], groups, [km[0, 0:1, :]], [km[0, 1:2, :]], acc_far, me * R)
-
-    def near_if(t):
-        @pl.when(t * 4 < me)
-        def _():
-            near(t, 0, NEAR_SLOTS)
-
-    def far_loop(first, n):
-        def body(t, carry):
-            far(t, first, n, 4)
-            return carry
-        lax.fori_loop((me + 1) // 4, PLANE // 4, body, 0)
-
-    pump(4, 1)
-    own_near()
-    near_if(0)
-    pump(5, 0)
-    near_if(1)
-    pump(5, 1)
-    near_if(2)
-    near_if(3)
-    pump(6, 0)
-    k_columns(9)
-    k_columns(10)
+    rest = jnp.maximum(row - 1, 0)
+    near_a = jnp.minimum(row + 1, 2)
+    near_b = near_a + (rest + 2) // 3
+    near_c = near_b + (rest + 1) // 3
+    near_loop(0, near_a)
+    pump(5)
+    k_columns(9, 2)
     far_loop(9, 2)
-    near_if(4)
-    pump(6, 1)
-    near_if(5)
-    pump(7, 0)
-    k_columns(11)
-    k_columns(12)
+    near_loop(near_a, near_b)
+    pump(6)
+    k_columns(11, 2)
     far_loop(11, 2)
-    near_if(6)
-    pump(7, 1)
-    near_if(7)
+    near_loop(near_b, near_c)
+    pump(7)
+    k_columns(13, 2)
+    far_loop(13, 2)
+    near_loop(near_c, row + 1)
+    own_far(9, 6)
 
     def back(s):
         d = (s + 1) // 2
@@ -369,17 +342,12 @@
         return rc(near_out.at[s], near_in.at[other], ns.at[s], nr.at[s], dev(dz=step))
 
     for s in range(NEAR_SLOTS):
-        near_out[s] = jnp.max(acc_near[:, s * R:(s + 1) * R], axis=0, keepdims=True)
+        near_out[s] = jnp.max(acc_near[s * R:(s + 1) * R, :].T, axis=0, keepdims=True)
     for s in range(1, NEAR_SLOTS):
         go(back(s))
-    k_columns(13)
-    k_columns(14)
-    far_loop(13, 2)
-    pump(8, 0)
-    pump(8, 1)
-    k_columns(15)
+    pump(8)
+    k_columns(15, 1)
     far_loop(15, 1)
-    own_far(NEAR_SLOTS, FAR_SLOTS)
 
     for s in range(PLANE):
         far_out[s] = jnp.max(acc_far[:, s * R:(s + 1) * R], axis=0, keepdims=True)
@@ -418,17 +386,15 @@
                 pltpu.VMEM((PLANE, R, D), jnp.bfloat16),
                 pltpu.VMEM((NZ, 2, R), f32),
                 pltpu.VMEM((PLANE, 2, R), f32),
-                pltpu.VMEM((PLANE * R, R), f32),
-                pltpu.VMEM((PLANE * R, R), f32),
-                pltpu.VMEM((FAR_SLOTS * R, R), f32),
-                pltpu.VMEM((FAR_SLOTS * R, R), f32),
-                pltpu.VMEM((8, NEAR_SLOTS * R), f32),
+                pltpu.VMEM((NZ * R, R), f32),
+                pltpu.VMEM((NZ * R, R), f32),
+                pltpu.VMEM((NEAR_SLOTS * R, R), f32),
                 pltpu.VMEM((8, PLANE * R), f32),
                 pltpu.VMEM((NEAR_SLOTS, 1, R), f32),
                 pltpu.VMEM((NEAR_SLOTS, 1, R), f32),
                 pltpu.VMEM((PLANE, 1, R), f32),
                 pltpu.VMEM((PLANE, 1, R), f32),
-                dma((32,)), dma((32,)), dma((16,)), dma((16,)),
+                dma((16,)), dma((16,)), dma((16,)), dma((16,)),
                 dma((40,)), dma((40,)), dma((15,)), dma((15,)),
                 dma((16,)), dma((16,)), dma((16,)), dma((16,)),
                 dma((NEAR_SLOTS,)), dma((NEAR_SLOTS,)), dma((PLANE,)), dma((PLANE,)),

time: 66.2 us -> 63.1 us (0.953)
  Pallas kernels: 65 us -> 61.8 us
    pallas_call x1, Pallas kernels: 65 us -> 61.8 us  [step(): pl.pallas_call(kernel, out_shape=jax.ShapeDtypeStruct((1, R), f32), in_sp...]
where the time goes in v2:
time: 63.1 us; the launch traced here: 62.9 us
  Pallas kernels  61.8 us (98%)
  local copies, waits for them, and re-layouts  1.1 us (2%)
    pallas_call x1, Pallas kernels, step(): pl.pallas_call(kernel, out_shape=jax.ShapeDtypeStruct((1, R), f32), in_sp...  61.8 us

profile of v2, /device:TPU:1, one launch (start us, length us, event | category | flops | bytes accessed | tf_op | source)
XLA Modules:
  0.0 62.9 jit_solution(14524967621730469556)
XLA Ops:
  0.0 61.8 %shard_map.37 = f32[1,128]{1,0:T(1,128)} custom-call(bf16[128,512]{1,0:T(8,128)(2,1)} %emb_ref.1, s32[1,128]{1,0:T(1,128)} %bitcast.4, s32[1,256]{1,0:T(1,128)} %bitcast.3), custom_call_target="tpu_custom_call" | custom-call | tf_op jit(solution)/shard_map/pallas_call | solution.py:379
  61.8 0.0 copy-start
  61.8 0.6 copy-done
  62.4 0.5 copy.5
Async XLA Ops:
  61.8 0.6 copy-start

commit v3 on v2

--- a/solution.py
+++ b/solution.py
@@ -15,6 +15,8 @@
 PLANE = NX * NY * NC
 TILE = 4 * R
 NT = (((1,), (1,)), ((), ()))
+CHUNKS = (0, 4, 4, 4, 4, 4, 1, 1, 1)
+START = tuple(2 * sum(CHUNKS[:d]) for d in range(NZ // 2 + 1))
 
 
 def kernel(
@@ -77,39 +79,42 @@
         pending.append(copy)
 
     half = R // 2
-
-    def ring(d, sign):
-        if sign > 0:
-            src, dst, lo = (0 if d == 1 else 2 * d - 3), 2 * d - 1, 0
+    way = 1 - 2 * c
+    twin = slot(0, 0, True)
+
+    def ring(d, o, part):
+        n = R // CHUNKS[d]
+        rows = pl.ds(part * n, n)
+        if d == 1:
+            src = kb.at[0, rows] if o == 0 else qb.at[twin, rows]
         else:
-            src, dst, lo = (0 if d == 1 else 2 * d - 2), min(2 * d, 15), half
-        i = (d - 1) * 2 + (0 if sign > 0 else 1)
-        rows = pl.ds(lo, half) if d == 8 else pl.ds(0, R)
-        return rc(kb.at[src, rows], kb.at[dst, rows], zs.at[i], zr.at[i], dev(dz=sign))
-
-    def ring_meta(d, sign):
-        if sign > 0:
-            src, dst = (0 if d == 1 else 2 * d - 3), 2 * d - 1
+            src = kb.at[2 * d - 3 + o, rows]
+        i = START[d] + o * CHUNKS[d] + part
+        return rc(src, kb.at[2 * d - 1 + o, rows], zs.at[i], zr.at[i], dev(dz=way))
+
+    def ring_meta(d, o):
+        if d == 1:
+            src = km.at[0] if o == 0 else qm.at[twin]
         else:
-            src, dst = (0 if d == 1 else 2 * d - 2), 2 * d
-        i = (d - 1) * 2 + (0 if sign > 0 else 1)
-        return rc(km.at[src], km.at[dst], zms.at[i], zmr.at[i], dev(dz=sign))
-
-    def forward(d):
-        for sign in (1, -1):
-            go(ring(d, sign))
-        for sign in (1, -1) if d < 8 else (1,):
-            go(ring_meta(d, sign))
-
-    def pump(d):
-        for sign in (1, -1):
-            ring(d, sign).wait_recv()
-            if d < 8:
-                go(ring(d + 1, sign))
-        for sign in (1, -1) if d < 8 else (1,):
-            ring_meta(d, sign).wait_recv()
-            if d < 7 or (d == 7 and sign > 0):
-                go(ring_meta(d + 1, sign))
+            src = km.at[2 * d - 3 + o]
+        i = 2 * d - 1 + o
+        return rc(src, km.at[i], zms.at[i], zmr.at[i], dev(dz=way))
+
+    def forward(d, o, lo, hi):
+        for part in range(CHUNKS[d]):
+            if lo < (part + 1) * (R // CHUNKS[d]) <= hi:
+                go(ring(d, o, part))
+
+    def pump(d, o):
+        ring_meta(d, o).wait_recv()
+        more = d < 7 or (d == 7 and o == 0)
+        if more:
+            go(ring_meta(d + 1, o))
+        n = R // CHUNKS[d]
+        for part in range(CHUNKS[d]):
+            ring(d, o, part).wait_recv()
+            if more:
+                forward(d + 1, o, part * n, (part + 1) * n)
 
     def move(h, phase, other, kind):
         along_x = (h == 0) == (phase == 0)
@@ -152,19 +157,8 @@
 
     pl.semaphore_wait(barrier, 7)
 
-    forward(1)
-    go(move_meta(0, 0, "+"))
-    go(move_meta(0, 0, "-"))
-    go(move_meta(1, 0, "+"))
-    go(move_meta(1, 0, "-"))
-    for h in range(2):
-        go(move(h, 0, 0, "+"))
-        go(move(h, 0, 0, "-"))
-    for h in range(2):
-        go(move(h, 1, 0, "+"))
-        go(move(h, 1, 0, "-"))
-    give(0, 0)
-    for sign, off in (("+", -1), ("-", 1)):
+    def line(off):
+        sign = "+" if off < 0 else "-"
         for h in range(2):
             move(h, 0, 0, sign).wait_recv()
             go(move(h, 0, 0, "f" + sign))
@@ -176,18 +170,42 @@
         for h in range(2):
             go(move(h, 1, off, "+"))
             go(move(h, 1, off, "-"))
-    pump(1)
-    for sign in ("+", "-"):
+
+    def cross(off):
+        for sign in ("+", "-"):
+            for h in range(2):
+                move(h, 1, off, sign).wait_recv()
+                go(move(h, 1, off, "f" + sign))
+            move_meta(1, off, sign).wait_recv()
+        go(move_meta(1, off, "f+"))
+
+    def cross_end(off):
         for h in range(2):
-            move(h, 1, 0, sign).wait_recv()
-            go(move(h, 1, 0, "f" + sign))
-        move_meta(1, 0, sign).wait_recv()
-        if sign == "+":
-            go(move_meta(1, 0, "f+"))
-    give(-1, 0)
-    give(1, 0)
-    give(0, -1)
-    give(0, 1)
+            for sign in ("+", "-"):
+                move(h, 1, off, "f" + sign).wait_recv()
+        move_meta(1, off, "f+").wait_recv()
+
+    go(ring_meta(1, 0))
+    give(0, 0)
+    forward(1, 0, 0, R)
+    for p in range(2):
+        go(move_meta(p, 0, "+"))
+        go(move_meta(p, 0, "-"))
+        for h in range(2):
+            go(move(h, p, 0, "+"))
+            go(move(h, p, 0, "-"))
+    for copy in share(0, 0):
+        copy.wait_recv()
+    go(ring_meta(1, 1))
+    forward(1, 1, 0, R)
+    pump(1, 0)
+    line(-1)
+    line(1)
+    pump(1, 1)
+    cross(0)
+    for dx, dy in ((-1, 0), (1, 0), (0, -1), (0, 1)):
+        give(dx, dy)
+    pump(2, 0)
     for h in range(2):
         for sign in ("+", "-"):
             move(h, 0, 0, "f" + sign).wait_recv()
@@ -197,40 +215,25 @@
     for h in range(2):
         go(move(h, 1, 2, "+"))
         go(move(h, 1, 2, "-"))
-    pump(2)
-    for off in (-1, 1):
-        for sign in ("+", "-"):
-            for h in range(2):
-                move(h, 1, off, sign).wait_recv()
-                go(move(h, 1, off, "f" + sign))
-            move_meta(1, off, sign).wait_recv()
-        go(move_meta(1, off, "f+"))
-    for h in range(2):
-        for sign in ("+", "-"):
-            move(h, 1, 0, "f" + sign).wait_recv()
-    move_meta(1, 0, "f+").wait_recv()
+    pump(2, 1)
+    cross(-1)
+    pump(3, 0)
+    cross(1)
+    cross_end(0)
     for dx, dy in ((-1, -1), (-1, 1), (1, -1), (1, 1), (2, 0), (0, 2)):
         give(dx, dy)
-    pump(3)
-    for sign in ("+", "-"):
-        for h in range(2):
-            move(h, 1, 2, sign).wait_recv()
-            go(move(h, 1, 2, "f" + sign))
-        move_meta(1, 2, sign).wait_recv()
-    go(move_meta(1, 2, "f+"))
-    for off in (-1, 1):
-        for h in range(2):
-            for sign in ("+", "-"):
-                move(h, 1, off, "f" + sign).wait_recv()
-        move_meta(1, off, "f+").wait_recv()
+    pump(3, 1)
+    pump(4, 0)
+    cross(2)
+    cross_end(-1)
+    cross_end(1)
     for dx, dy in ((2, -1), (2, 1), (-1, 2), (1, 2)):
         give(dx, dy)
-    for h in range(2):
-        for sign in ("+", "-"):
-            move(h, 1, 2, "f" + sign).wait_recv()
-    move_meta(1, 2, "f+").wait_recv()
+    pump(4, 1)
+    cross_end(2)
     give(2, 2)
-    pump(4)
+    pump(5, 0)
+    pump(5, 1)
     acc_near[...] = jnp.full(acc_near.shape, -1.0, jnp.float32)
     acc_far[...] = jnp.full(acc_far.shape, -1.0, jnp.float32)
 
@@ -245,7 +248,28 @@
         score = jnp.where(s_cl == l_cl, s, 0.5 * s)
         return jnp.where(s_gr == l_gr, score, -1.0)
 
-    def near(t):
+    def block(s):
+        if s == 0:
+            return me, z
+        d = (s + 1) // 2
+        return (me if s % 2 else twin), (z - d * way) & 15
+
+    before = sub > lax.broadcasted_iota(jnp.int32, (R, R), 1)
+
+    def groups(q, first, n, near_side):
+        out = []
+        for s in range(first, first + n):
+            nk, zk = block(s)
+            if not near_side:
+                ok = (q > nk) | ((q == nk) & (z > zk))
+            elif s == 0:
+                ok = (q < nk) | ((q == nk) & before)
+            else:
+                ok = (q < nk) | ((q == nk) & (zk > z))
+            out.append(jnp.where(ok, kgr[s * R:(s + 1) * R, :], -1.0))
+        return jnp.concatenate(out, axis=0) if n > 1 else out[0]
+
+    def near(t, edge):
         stream = kb[0:NEAR_SLOTS].reshape(NEAR_SLOTS * R, D)
         lanes = qb[pl.ds(t * 4, 4)].reshape(TILE, D)
         sims = lax.dot_general(stream, lanes, NT, preferred_element_type=jnp.float32)
@@ -253,99 +277,67 @@
         best = acc_near[...]
         for j in range(4):
             q = t * 4 + j
-            gr = jnp.where(q < me, qm[q, 1:2, :], -2.0)
-            best = jnp.maximum(best, scores(sims, j, kcl[rows, :], kgr[rows, :], qm[q, 0:1, :], gr))
+            gr = groups(q, 0, NEAR_SLOTS, True) if edge else kgr[rows, :]
+            best = jnp.maximum(best, scores(sims, j, kcl[rows, :], gr, qm[q, 0:1, :], qm[q, 1:2, :]))
         acc_near[...] = best
 
-    def near_loop(lo, hi):
+    def near_loop(lo, hi, edge=False):
         def body(t, carry):
-            near(t)
+            near(t, edge)
             return carry
         lax.fori_loop(lo, hi, body, 0)
 
-    def origin(s):
-        if s == 0:
-            return z
-        d = (s + 1) // 2
-        return (z - d) & 15 if s % 2 else (z + d) & 15
-
-    def own_near():
-        stream = kb[0:NEAR_SLOTS].reshape(NEAR_SLOTS * R, D)
-        sims = lax.dot_general(stream, kb[0], NT, preferred_element_type=jnp.float32)
-        rows = pl.ds(0, NEAR_SLOTS * R)
-        lane = lax.broadcasted_iota(jnp.int32, (R, R), 1)
-        groups = [jnp.where(sub > lane, kgr[0:R, :], -1.0)]
-        for s in range(1, NEAR_SLOTS):
-            groups.append(jnp.where(origin(s) > z, kgr[s * R:(s + 1) * R, :], -1.0))
-        acc_near[...] = jnp.maximum(acc_near[...], scores(
-            sims, 0, kcl[rows, :], jnp.concatenate(groups, axis=0), km[0, 0:1, :], km[0, 1:2, :]))
-
-    def into_far(best, s):
-        where = pl.ds(pl.multiple_of(s * R, R), R)
-        n = best.shape[0] // 8
-        acc_far[:, where] = jnp.maximum(acc_far[:, where], jnp.max(best.reshape(n, 8, R), axis=0))
-
-    def far(t, first, n):
+    def far(t, first, n, edge):
         rows = pl.ds(first * R, n * R)
         stream = kb[first:first + n].reshape(n * R, D)
         lanes = qb[pl.ds(t * 8, 8)].reshape(2 * TILE, D)
         sims = lax.dot_general(stream, lanes, NT, preferred_element_type=jnp.float32)
         for j in range(8):
             q = t * 8 + j
-            later = q > me
-            if n == 1:
-                later = later | ((q == me) & (origin(first) < z))
-            gr = jnp.where(later, qm[q, 1:2, :], -2.0)
-            into_far(scores(sims, j, kcl[rows, :], kgr[rows, :], qm[q, 0:1, :], gr), q)
+            gr = groups(q, first, n, False) if edge else kgr[rows, :]
+            best = scores(sims, j, kcl[rows, :], gr, qm[q, 0:1, :], qm[q, 1:2, :])
+            where = pl.ds(pl.multiple_of(q * R, R), R)
+            acc_far[:, where] = jnp.maximum(acc_far[:, where], jnp.max(best.reshape(n * R // 8, 8, R), axis=0))
 
     def far_loop(first, n):
+        far(y, first, n, True)
         def body(t, carry):
-            far(t, first, n)
+            far(t, first, n, False)
             return carry
-        lax.fori_loop(me // 8, PLANE // 8, body, 0)
-
-    def own_far(first, n):
-        stream = kb[first:first + n].reshape(n * R, D)
-        sims = lax.dot_general(stream, kb[0], NT, preferred_element_type=jnp.float32)
-        groups = jnp.concatenate(
-            [jnp.where(origin(s) < z, kgr[s * R:(s + 1) * R, :], -1.0) for s in range(first, first + n)], axis=0)
-        into_far(scores(sims, 0, kcl[pl.ds(first * R, n * R), :], groups, km[0, 0:1, :], km[0, 1:2, :]), me)
-
-    k_columns(0, NEAR_SLOTS)
-    own_near()
+        lax.fori_loop(y + 1, NY, body, 0)
+
+    k_columns(0, 11)
     for dy in range(NY):
         for dx in range(NX):
-            for copy in share(dx, dy):
-                copy.wait_recv()
-    rest = jnp.maximum(row - 1, 0)
-    near_a = jnp.minimum(row + 1, 2)
-    near_b = near_a + (rest + 2) // 3
-    near_c = near_b + (rest + 1) // 3
-    near_loop(0, near_a)
-    pump(5)
-    k_columns(9, 2)
+            if dx or dy:
+                for copy in share(dx, dy):
+                    copy.wait_recv()
+    cut_a = y // 2
+    cut_b = cut_a + (2 * y - cut_a + 1) // 2
+    near_loop(2 * y, 2 * y + 2, True)
+    near_loop(0, cut_a)
     far_loop(9, 2)
-    near_loop(near_a, near_b)
-    pump(6)
+    pump(6, 0)
+    pump(6, 1)
     k_columns(11, 2)
+    near_loop(cut_a, cut_b)
     far_loop(11, 2)
-    near_loop(near_b, near_c)
-    pump(7)
+    pump(7, 0)
+    pump(7, 1)
     k_columns(13, 2)
+    near_loop(cut_b, 2 * y)
     far_loop(13, 2)
-    near_loop(near_c, row + 1)
-    own_far(9, 6)
 
     def back(s):
-        d = (s + 1) // 2
-        step, other = (-d, 2 * d) if s % 2 else (d, 2 * d - 1)
-        return rc(near_out.at[s], near_in.at[other], ns.at[s], nr.at[s], dev(dz=step))
+        d, o = (s + 1) // 2, (s + 1) % 2
+        at = 2 * d - 1 + c
+        return rc(near_out.at[s], near_in.at[at], ns.at[s], nr.at[at], dev(dz=-d * way, flip=o == 1))
 
     for s in range(NEAR_SLOTS):
         near_out[s] = jnp.max(acc_near[s * R:(s + 1) * R, :].T, axis=0, keepdims=True)
     for s in range(1, NEAR_SLOTS):
         go(back(s))
-    pump(8)
+    pump(8, 0)
     k_columns(15, 1)
     far_loop(15, 1)
 
@@ -360,7 +352,7 @@
         go(reply(k))
     best = jnp.maximum(near_out[0], far_out[me])
     for s in range(1, NEAR_SLOTS):
-        back(s).wait_recv()
+        rc(near_out.at[0], near_in.at[s], ns.at[0], nr.at[s], dev(dz=1)).wait_recv()
     for s in range(1, NEAR_SLOTS):
         best = jnp.maximum(best, near_in[s])
     for k in range(1, PLANE):
@@ -394,7 +386,7 @@
                 pltpu.VMEM((NEAR_SLOTS, 1, R), f32),
                 pltpu.VMEM((PLANE, 1, R), f32),
                 pltpu.VMEM((PLANE, 1, R), f32),
-                dma((16,)), dma((16,)), dma((16,)), dma((16,)),
+                dma((2 * sum(CHUNKS),)), dma((2 * sum(CHUNKS),)), dma((NZ,)), dma((NZ,)),
                 dma((40,)), dma((40,)), dma((15,)), dma((15,)),
                 dma((16,)), dma((16,)), dma((16,)), dma((16,)),
                 dma((NEAR_SLOTS,)), dma((NEAR_SLOTS,)), dma((PLANE,)), dma((PLANE,)),

time: 63.1 us -> 58.6 us (0.929)
  Pallas kernels: 61.8 us -> 57.4 us
    pallas_call x1, Pallas kernels: 61.8 us -> 57.4 us  [step(): pl.pallas_call(kernel, out_shape=jax.ShapeDtypeStruct((1, R), f32), in_sp...]
where the time goes in v3:
time: 58.6 us; the launch traced here: 58.5 us
  Pallas kernels  57.4 us (98%)
  local copies, waits for them, and re-layouts  1.1 us (2%)
    pallas_call x1, Pallas kernels, step(): pl.pallas_call(kernel, out_shape=jax.ShapeDtypeStruct((1, R), f32), in_sp...  57.4 us

profile of v3, /device:TPU:1, one launch (start us, length us, event | category | flops | bytes accessed | tf_op | source)
XLA Modules:
  0.0 58.5 jit_solution(7179330219943102056)
XLA Ops:
  0.0 57.4 %shard_map.37 = f32[1,128]{1,0:T(1,128)} custom-call(bf16[128,512]{1,0:T(8,128)(2,1)} %emb_ref.1, s32[1,128]{1,0:T(1,128)} %bitcast.4, s32[1,256]{1,0:T(1,128)} %bitcast.3), custom_call_target="tpu_custom_call" | custom-call | tf_op jit(solution)/shard_map/pallas_call | solution.py:371
  57.4 0.0 copy-start
  57.4 0.6 %copy-done = f32[1,128]{1,0:T(1,128)S(1)} copy-done((f32[1,128]{1,0:T(1,128)S(1)}, f32[1,128]{1,0:T(1,128)}, u32[]{:S(2)}) %copy-start) | copy-done | bytes 536
  58.0 0.5 copy.5
Async XLA Ops:
  57.4 0.6 %copy-start = (f32[1,128]{1,0:T(1,128)S(1)}, f32[1,128]{1,0:T(1,128)}, u32[]{:S(2)}) copy-start(f32[1,128]{1,0:T(1,128)} %shard_map.37) | copy-start | bytes 1540

commit v4 on v3

--- a/solution.py
+++ b/solution.py
@@ -12,6 +12,7 @@
 R, D = 128, 512
 NEAR = 4
 NEAR_SLOTS = 2 * NEAR + 1
+FAR_SLOTS = NZ - NEAR_SLOTS
 PLANE = NX * NY * NC
 TILE = 4 * R
 NT = (((1,), (1,)), ((), ()))
@@ -20,10 +21,10 @@
 
 
 def kernel(
-    emb_ref, cid_ref, table_ref, out_ref,
-    kb, qb, km, qm, kcl, kgr, acc_near, acc_far,
-    near_out, near_in, far_out, far_in,
-    zs, zr, zms, zmr, qs, qr, qms, qmr, ds, dr, dms, dmr, ns, nr, fs, fr,
+    emb_hbm, cid_hbm, table_hbm, out_ref,
+    emb_ref, cid_ref, table_ref, kb, qb, km, qm, kcl, kgr, acc_q, acc_k,
+    k_out, k_in, q_out, q_in,
+    ins, zs, zr, zms, zmr, qs, qr, qms, qmr, ds, dr, dms, dmr, ns, nr, fs, fr,
 ):
     clu, grp = lax.axis_index("clu"), lax.axis_index("grp")
     x, z = clu // NZ, clu % NZ
@@ -40,34 +41,20 @@
         cc = 1 - c if flip else c
         return (((y + dy) & 3) * NC + cc) * NX + ((x + dx) & 3)
 
+    fetch = [pltpu.make_async_copy(a, b, ins.at[i]) for i, (a, b) in enumerate(
+        ((emb_hbm, emb_ref), (cid_hbm, cid_ref), (table_hbm, table_ref)))]
+    for copy in fetch:
+        copy.start()
     barrier = pltpu.get_barrier_semaphore()
     for step in (dict(dx=1), dict(dx=-1), dict(dy=1), dict(dy=-1), dict(dz=1), dict(dz=-1), dict(flip=True)):
         pl.semaphore_signal(barrier, inc=1, device_id=dev(**step), device_id_type=MESH)
 
+    fetch[0].wait()
     values = emb_ref[...].astype(jnp.float32)
     scale = lax.rsqrt(jnp.sum(values * values, axis=1, keepdims=True) + 1e-06)
     unit = (values * scale).astype(jnp.bfloat16)
     kb[0] = unit
     qb[me] = unit
-    eye = lax.broadcasted_iota(jnp.int32, (R, R), 0) == lax.broadcasted_iota(jnp.int32, (R, R), 1)
-    sub = lax.broadcasted_iota(jnp.int32, (R, R), 0)
-    ones = jnp.ones((R, R), jnp.bfloat16)
-
-    def column(line):
-        spread = jnp.where(eye, jnp.broadcast_to(line, (R, R)), 0.0).astype(jnp.bfloat16)
-        return jnp.dot(spread, ones, preferred_element_type=jnp.float32)
-
-    cid = cid_ref[...]
-    group = jnp.zeros((1, R), jnp.float32)
-    for h in range(2):
-        part = column(table_ref[:, h * R:(h + 1) * R].astype(jnp.float32))
-        group += jnp.sum(jnp.where(jnp.broadcast_to(cid, (R, R)) == sub + h * R, part, 0.0), axis=0, keepdims=True)
-    cluster = cid.astype(jnp.float32)
-    km[0, 0:1, :] = cluster
-    km[0, 1:2, :] = group
-    qm[me, 0:1, :] = cluster
-    qm[me, 1:2, :] = group
-
     pending = []
 
     def rc(src, dst, s, r, where):
@@ -155,7 +142,6 @@
         for copy in share(dx, dy):
             go(copy)
 
-    pl.semaphore_wait(barrier, 7)
 
     def line(off):
         sign = "+" if off < 0 else "-"
@@ -185,27 +171,54 @@
                 move(h, 1, off, "f" + sign).wait_recv()
         move_meta(1, off, "f+").wait_recv()
 
+    pl.semaphore_wait(barrier, 7)
+    own_share = share(0, 0)
+    go(own_share[0])
+    forward(1, 0, 0, R)
+    for p in range(2):
+        for h in range(2):
+            go(move(h, p, 0, "+"))
+            go(move(h, p, 0, "-"))
+
+    fetch[1].wait()
+    fetch[2].wait()
+    eye = lax.broadcasted_iota(jnp.int32, (R, R), 0) == lax.broadcasted_iota(jnp.int32, (R, R), 1)
+    sub = lax.broadcasted_iota(jnp.int32, (R, R), 0)
+    ones = jnp.ones((R, R), jnp.bfloat16)
+
+    def column(line):
+        spread = jnp.where(eye, jnp.broadcast_to(line, (R, R)), 0.0).astype(jnp.bfloat16)
+        return jnp.dot(spread, ones, preferred_element_type=jnp.float32)
+
+    cid = cid_ref[...]
+    group = jnp.zeros((1, R), jnp.float32)
+    for h in range(2):
+        part = column(table_ref[:, h * R:(h + 1) * R].astype(jnp.float32))
+        group += jnp.sum(jnp.where(jnp.broadcast_to(cid, (R, R)) == sub + h * R, part, 0.0), axis=0, keepdims=True)
+    cluster = cid.astype(jnp.float32)
+    km[0, 0:1, :] = cluster
+    km[0, 1:2, :] = group
+    qm[me, 0:1, :] = cluster
+    qm[me, 1:2, :] = group
+
+    go(own_share[1])
     go(ring_meta(1, 0))
-    give(0, 0)
-    forward(1, 0, 0, R)
     for p in range(2):
         go(move_meta(p, 0, "+"))
         go(move_meta(p, 0, "-"))
-        for h in range(2):
-            go(move(h, p, 0, "+"))
-            go(move(h, p, 0, "-"))
-    for copy in share(0, 0):
-        copy.wait_recv()
+    own_share[0].wait_recv()
+    forward(1, 1, 0, R)
+    own_share[1].wait_recv()
     go(ring_meta(1, 1))
-    forward(1, 1, 0, R)
     pump(1, 0)
+    pump(1, 1)
     line(-1)
     line(1)
-    pump(1, 1)
+    pump(2, 0)
     cross(0)
     for dx, dy in ((-1, 0), (1, 0), (0, -1), (0, 1)):
         give(dx, dy)
-    pump(2, 0)
+    pump(2, 1)
     for h in range(2):
         for sign in ("+", "-"):
             move(h, 0, 0, "f" + sign).wait_recv()
@@ -215,7 +228,6 @@
     for h in range(2):
         go(move(h, 1, 2, "+"))
         go(move(h, 1, 2, "-"))
-    pump(2, 1)
     cross(-1)
     pump(3, 0)
     cross(1)
@@ -230,12 +242,8 @@
     for dx, dy in ((2, -1), (2, 1), (-1, 2), (1, 2)):
         give(dx, dy)
     pump(4, 1)
-    cross_end(2)
-    give(2, 2)
-    pump(5, 0)
-    pump(5, 1)
-    acc_near[...] = jnp.full(acc_near.shape, -1.0, jnp.float32)
-    acc_far[...] = jnp.full(acc_far.shape, -1.0, jnp.float32)
+    acc_q[...] = jnp.full(acc_q.shape, -1.0, jnp.float32)
+    acc_k[...] = jnp.full(acc_k.shape, -1.0, jnp.float32)
 
     def k_columns(first, n):
         for s in range(first, first + n):
@@ -254,18 +262,18 @@
         d = (s + 1) // 2
         return (me if s % 2 else twin), (z - d * way) & 15
 
-    before = sub > lax.broadcasted_iota(jnp.int32, (R, R), 1)
+    before = sub < lax.broadcasted_iota(jnp.int32, (R, R), 1)
 
     def groups(q, first, n, near_side):
         out = []
         for s in range(first, first + n):
             nk, zk = block(s)
             if not near_side:
+                ok = (q < nk) | ((q == nk) & (zk > z))
+            elif s == 0:
+                ok = (q > nk) | ((q == nk) & before)
+            else:
                 ok = (q > nk) | ((q == nk) & (z > zk))
-            elif s == 0:
-                ok = (q < nk) | ((q == nk) & before)
-            else:
-                ok = (q < nk) | ((q == nk) & (zk > z))
             out.append(jnp.where(ok, kgr[s * R:(s + 1) * R, :], -1.0))
         return jnp.concatenate(out, axis=0) if n > 1 else out[0]
 
@@ -274,12 +282,12 @@
         lanes = qb[pl.ds(t * 4, 4)].reshape(TILE, D)
         sims = lax.dot_general(stream, lanes, NT, preferred_element_type=jnp.float32)
         rows = pl.ds(0, NEAR_SLOTS * R)
-        best = acc_near[...]
         for j in range(4):
             q = t * 4 + j
             gr = groups(q, 0, NEAR_SLOTS, True) if edge else kgr[rows, :]
-            best = jnp.maximum(best, scores(sims, j, kcl[rows, :], gr, qm[q, 0:1, :], qm[q, 1:2, :]))
-        acc_near[...] = best
+            best = scores(sims, j, kcl[rows, :], gr, qm[q, 0:1, :], qm[q, 1:2, :])
+            where = pl.ds(pl.multiple_of(q * R, R), R)
+            acc_q[:, where] = jnp.max(best.reshape(NEAR_SLOTS * R // 8, 8, R), axis=0)
 
     def near_loop(lo, hi, edge=False):
         def body(t, carry):
@@ -292,73 +300,81 @@
         stream = kb[first:first + n].reshape(n * R, D)
         lanes = qb[pl.ds(t * 8, 8)].reshape(2 * TILE, D)
         sims = lax.dot_general(stream, lanes, NT, preferred_element_type=jnp.float32)
+        at = pl.ds((first - NEAR_SLOTS) * R, n * R)
+        best = acc_k[at, :]
         for j in range(8):
             q = t * 8 + j
             gr = groups(q, first, n, False) if edge else kgr[rows, :]
-            best = scores(sims, j, kcl[rows, :], gr, qm[q, 0:1, :], qm[q, 1:2, :])
-            where = pl.ds(pl.multiple_of(q * R, R), R)
-            acc_far[:, where] = jnp.maximum(acc_far[:, where], jnp.max(best.reshape(n * R // 8, 8, R), axis=0))
+            best = jnp.maximum(best, scores(sims, j, kcl[rows, :], gr, qm[q, 0:1, :], qm[q, 1:2, :]))
+        acc_k[at, :] = best
 
     def far_loop(first, n):
-        far(y, first, n, True)
         def body(t, carry):
             far(t, first, n, False)
             return carry
-        lax.fori_loop(y + 1, NY, body, 0)
-
-    k_columns(0, 11)
-    for dy in range(NY):
+        lax.fori_loop(0, y, body, 0)
+        far(y, first, n, True)
+
+    def back(s):
+        d, o = (s + 1) // 2, (s + 1) % 2
+        at = 2 * (d - NEAR - 1) + (c if d < 8 else 0)
+        i = s - NEAR_SLOTS
+        return rc(k_out.at[i], k_in.at[at], ns.at[i], nr.at[at], dev(dz=-d * way, flip=o == 1))
+
+    def send_back(first, n):
+        for s in range(first, first + n):
+            i = s - NEAR_SLOTS
+            k_out[i] = jnp.max(acc_k[i * R:(i + 1) * R, :].T, axis=0, keepdims=True)
+            go(back(s))
+
+    def reply(k):
+        dx, dy, flip = k % NX, (k // NX) % NY, k >= NX * NY
+        return rc(q_out.at[slot(dx, dy, flip)], q_in.at[k], fs.at[k], fr.at[k], dev(dx, dy, 0, flip))
+
+    k_columns(0, NEAR_SLOTS)
+    for dx in range(1, NX):
+        for copy in share(dx, 0):
+            copy.wait_recv()
+    near_loop(2 * y, 2 * y + 2, True)
+    cross_end(2)
+    give(2, 2)
+    pump(5, 0)
+    pump(5, 1)
+    k_columns(9, 2)
+    for dy in range(1, NY):
         for dx in range(NX):
-            if dx or dy:
-                for copy in share(dx, dy):
-                    copy.wait_recv()
-    cut_a = y // 2
-    cut_b = cut_a + (2 * y - cut_a + 1) // 2
-    near_loop(2 * y, 2 * y + 2, True)
-    near_loop(0, cut_a)
+            for copy in share(dx, dy):
+                copy.wait_recv()
+    cut = 2 * y + 2 + (6 - 2 * y) // 2
+    near_loop(2 * y + 2, cut)
     far_loop(9, 2)
     pump(6, 0)
     pump(6, 1)
     k_columns(11, 2)
-    near_loop(cut_a, cut_b)
-    far_loop(11, 2)
+    near_loop(cut, PLANE // 4)
+    for s in range(PLANE):
+        q_out[s] = jnp.max(acc_q[:, s * R:(s + 1) * R], axis=0, keepdims=True)
     pump(7, 0)
     pump(7, 1)
+    for k in range(1, PLANE):
+        go(reply(k))
+    far_loop(11, 2)
     k_columns(13, 2)
-    near_loop(cut_b, 2 * y)
     far_loop(13, 2)
-
-    def back(s):
-        d, o = (s + 1) // 2, (s + 1) % 2
-        at = 2 * d - 1 + c
-        return rc(near_out.at[s], near_in.at[at], ns.at[s], nr.at[at], dev(dz=-d * way, flip=o == 1))
-
-    for s in range(NEAR_SLOTS):
-        near_out[s] = jnp.max(acc_near[s * R:(s + 1) * R, :].T, axis=0, keepdims=True)
-    for s in range(1, NEAR_SLOTS):
-        go(back(s))
+    send_back(9, 6)
+    best = q_out[me]
+    for k in range(1, PLANE):
+        reply(k).wait_recv()
+    for k in range(1, PLANE):
+        best = jnp.maximum(best, q_in[k])
     pump(8, 0)
     k_columns(15, 1)
     far_loop(15, 1)
-
-    for s in range(PLANE):
-        far_out[s] = jnp.max(acc_far[:, s * R:(s + 1) * R], axis=0, keepdims=True)
-
-    def reply(k):
-        dx, dy, flip = k % NX, (k // NX) % NY, k >= NX * NY
-        return rc(far_out.at[slot(dx, dy, flip)], far_in.at[k], fs.at[k], fr.at[k], dev(dx, dy, 0, flip))
-
-    for k in range(1, PLANE):
-        go(reply(k))
-    best = jnp.maximum(near_out[0], far_out[me])
-    for s in range(1, NEAR_SLOTS):
-        rc(near_out.at[0], near_in.at[s], ns.at[0], nr.at[s], dev(dz=1)).wait_recv()
-    for s in range(1, NEAR_SLOTS):
-        best = jnp.maximum(best, near_in[s])
-    for k in range(1, PLANE):
-        reply(k).wait_recv()
-    for k in range(1, PLANE):
-        best = jnp.maximum(best, far_in[k])
+    send_back(15, 1)
+    for s in range(FAR_SLOTS):
+        rc(k_out.at[0], k_in.at[s], ns.at[0], nr.at[s], dev(dz=1)).wait_recv()
+    for s in range(FAR_SLOTS):
+        best = jnp.maximum(best, k_in[s])
     out_ref[...] = best
     for copy in pending:
         copy.wait_send()
@@ -371,25 +387,29 @@
         best = pl.pallas_call(
             kernel,
             out_shape=jax.ShapeDtypeStruct((1, R), f32),
-            in_specs=[pl.BlockSpec(memory_space=pltpu.VMEM)] * 3,
+            in_specs=[pl.BlockSpec(memory_space=pl.ANY)] * 3,
             out_specs=pl.BlockSpec(memory_space=pltpu.VMEM),
             scratch_shapes=[
+                pltpu.VMEM((R, D), jnp.bfloat16),
+                pltpu.VMEM((1, R), jnp.int32),
+                pltpu.VMEM((1, cluster_group.shape[0]), jnp.int32),
                 pltpu.VMEM((NZ, R, D), jnp.bfloat16),
                 pltpu.VMEM((PLANE, R, D), jnp.bfloat16),
                 pltpu.VMEM((NZ, 2, R), f32),
                 pltpu.VMEM((PLANE, 2, R), f32),
                 pltpu.VMEM((NZ * R, R), f32),
                 pltpu.VMEM((NZ * R, R), f32),
-                pltpu.VMEM((NEAR_SLOTS * R, R), f32),
                 pltpu.VMEM((8, PLANE * R), f32),
-                pltpu.VMEM((NEAR_SLOTS, 1, R), f32),
-                pltpu.VMEM((NEAR_SLOTS, 1, R), f32),
+                pltpu.VMEM((FAR_SLOTS * R, R), f32),
+                pltpu.VMEM((FAR_SLOTS, 1, R), f32),
+                pltpu.VMEM((FAR_SLOTS, 1, R), f32),
                 pltpu.VMEM((PLANE, 1, R), f32),
                 pltpu.VMEM((PLANE, 1, R), f32),
+                dma((3,)),
                 dma((2 * sum(CHUNKS),)), dma((2 * sum(CHUNKS),)), dma((NZ,)), dma((NZ,)),
                 dma((40,)), dma((40,)), dma((15,)), dma((15,)),
                 dma((16,)), dma((16,)), dma((16,)), dma((16,)),
-                dma((NEAR_SLOTS,)), dma((NEAR_SLOTS,)), dma((PLANE,)), dma((PLANE,)),
+                dma((FAR_SLOTS,)), dma((FAR_SLOTS,)), dma((PLANE,)), dma((PLANE,)),
             ],
             compiler_params=pltpu.CompilerParams(
                 collective_id=0, has_side_effects=True, vmem_limit_bytes=60 * 2**20),

time: 58.6 us -> 59.6 us (1.017)
  the two profiles are of different devices: /device:TPU:1 before, /device:TPU:24 now
where the time goes in v4:
time: 59.6 us; the launch traced here: 59.5 us
  Pallas kernels  58.3 us (98%)
  local copies, waits for them, and re-layouts  1.1 us (2%)
    pallas_call x1, Pallas kernels, step(): pl.pallas_call(kernel, out_shape=jax.ShapeDtypeStruct((1, R), f32), in_sp...  58.3 us

profile of v4, /device:TPU:24, one launch (start us, length us, event | category | flops | bytes accessed | tf_op | source)
XLA Modules:
  0.0 59.5 jit_solution(7659500656785418883)
XLA Ops:
  0.0 58.3 %shard_map.37 = f32[1,128]{1,0:T(1,128)} custom-call(bf16[128,512]{1,0:T(8,128)(2,1)} %emb_hbm.1, s32[1,128]{1,0:T(1,128)} %bitcast.4, s32[1,256]{1,0:T(1,128)} %bitcast.3), custom_call_target="tpu_custom_call" | custom-call | tf_op jit(solution)/shard_map/pallas_call | solution.py:387
  58.4 0.0 copy-start
  58.4 0.6 copy-done
  59.0 0.5 copy.5
Async XLA Ops:
  58.4 0.6 %copy-start = (f32[1,128]{1,0:T(1,128)S(1)}, f32[1,128]{1,0:T(1,128)}, u32[]{:S(2)}) copy-start(f32[1,128]{1,0:T(1,128)} %shard_map.37) | copy-start | bytes 1540

commit v5 on v4

--- a/solution.py
+++ b/solution.py
@@ -12,7 +12,6 @@
 R, D = 128, 512
 NEAR = 4
 NEAR_SLOTS = 2 * NEAR + 1
-FAR_SLOTS = NZ - NEAR_SLOTS
 PLANE = NX * NY * NC
 TILE = 4 * R
 NT = (((1,), (1,)), ((), ()))
@@ -262,36 +261,36 @@
         d = (s + 1) // 2
         return (me if s % 2 else twin), (z - d * way) & 15
 
-    before = sub < lax.broadcasted_iota(jnp.int32, (R, R), 1)
+    before = sub > lax.broadcasted_iota(jnp.int32, (R, R), 1)
 
     def groups(q, first, n, near_side):
         out = []
         for s in range(first, first + n):
             nk, zk = block(s)
             if not near_side:
+                ok = (q > nk) | ((q == nk) & (z > zk))
+            elif s == 0:
+                ok = (q < nk) | ((q == nk) & before)
+            else:
                 ok = (q < nk) | ((q == nk) & (zk > z))
-            elif s == 0:
-                ok = (q > nk) | ((q == nk) & before)
-            else:
-                ok = (q > nk) | ((q == nk) & (z > zk))
             out.append(jnp.where(ok, kgr[s * R:(s + 1) * R, :], -1.0))
         return jnp.concatenate(out, axis=0) if n > 1 else out[0]
 
     def near(t, edge):
         stream = kb[0:NEAR_SLOTS].reshape(NEAR_SLOTS * R, D)
-        lanes = qb[pl.ds(t * 4, 4)].reshape(TILE, D)
+        lanes = qb[pl.ds(t * 8, 8)].reshape(2 * TILE, D)
         sims = lax.dot_general(stream, lanes, NT, preferred_element_type=jnp.float32)
         rows = pl.ds(0, NEAR_SLOTS * R)
-        for j in range(4):
-            q = t * 4 + j
+        best = acc_k[...]
+        for j in range(8):
+            q = t * 8 + j
             gr = groups(q, 0, NEAR_SLOTS, True) if edge else kgr[rows, :]
-            best = scores(sims, j, kcl[rows, :], gr, qm[q, 0:1, :], qm[q, 1:2, :])
-            where = pl.ds(pl.multiple_of(q * R, R), R)
-            acc_q[:, where] = jnp.max(best.reshape(NEAR_SLOTS * R // 8, 8, R), axis=0)
-
-    def near_loop(lo, hi, edge=False):
+            best = jnp.maximum(best, scores(sims, j, kcl[rows, :], gr, qm[q, 0:1, :], qm[q, 1:2, :]))
+        acc_k[...] = best
+
+    def near_loop(lo, hi):
         def body(t, carry):
-            near(t, edge)
+            near(t, False)
             return carry
         lax.fori_loop(lo, hi, body, 0)
 
@@ -300,42 +299,43 @@
         stream = kb[first:first + n].reshape(n * R, D)
         lanes = qb[pl.ds(t * 8, 8)].reshape(2 * TILE, D)
         sims = lax.dot_general(stream, lanes, NT, preferred_element_type=jnp.float32)
-        at = pl.ds((first - NEAR_SLOTS) * R, n * R)
-        best = acc_k[at, :]
         for j in range(8):
             q = t * 8 + j
             gr = groups(q, first, n, False) if edge else kgr[rows, :]
-            best = jnp.maximum(best, scores(sims, j, kcl[rows, :], gr, qm[q, 0:1, :], qm[q, 1:2, :]))
-        acc_k[at, :] = best
+            best = scores(sims, j, kcl[rows, :], gr, qm[q, 0:1, :], qm[q, 1:2, :])
+            where = pl.ds(pl.multiple_of(q * R, R), R)
+            acc_q[:, where] = jnp.maximum(acc_q[:, where], jnp.max(best.reshape(n * R // 8, 8, R), axis=0))
 
     def far_loop(first, n):
         def body(t, carry):
             far(t, first, n, False)
             return carry
-        lax.fori_loop(0, y, body, 0)
+        lax.fori_loop(y + 1, NY, body, 0)
         far(y, first, n, True)
 
     def back(s):
         d, o = (s + 1) // 2, (s + 1) % 2
-        at = 2 * (d - NEAR - 1) + (c if d < 8 else 0)
-        i = s - NEAR_SLOTS
-        return rc(k_out.at[i], k_in.at[at], ns.at[i], nr.at[at], dev(dz=-d * way, flip=o == 1))
-
-    def send_back(first, n):
-        for s in range(first, first + n):
-            i = s - NEAR_SLOTS
-            k_out[i] = jnp.max(acc_k[i * R:(i + 1) * R, :].T, axis=0, keepdims=True)
-            go(back(s))
+        at = 2 * d - 1 + c
+        return rc(k_out.at[s], k_in.at[at], ns.at[s], nr.at[at], dev(dz=-d * way, flip=o == 1))
 
     def reply(k):
         dx, dy, flip = k % NX, (k // NX) % NY, k >= NX * NY
         return rc(q_out.at[slot(dx, dy, flip)], q_in.at[k], fs.at[k], fr.at[k], dev(dx, dy, 0, flip))
+
+    def hops(k):
+        dx, dy = k % NX, (k // NX) % NY
+        return min(dx, NX - dx) + min(dy, NY - dy)
+
+    def plane_result(k):
+        dx, dy, flip = k % NX, (k // NX) % NY, k >= NX * NY
+        s = slot(dx, dy, flip)
+        return s, jnp.max(acc_q[:, pl.ds(pl.multiple_of(s * R, R), R)], axis=0, keepdims=True)
 
     k_columns(0, NEAR_SLOTS)
     for dx in range(1, NX):
         for copy in share(dx, 0):
             copy.wait_recv()
-    near_loop(2 * y, 2 * y + 2, True)
+    near(y, True)
     cross_end(2)
     give(2, 2)
     pump(5, 0)
@@ -345,36 +345,40 @@
         for dx in range(NX):
             for copy in share(dx, dy):
                 copy.wait_recv()
-    cut = 2 * y + 2 + (6 - 2 * y) // 2
-    near_loop(2 * y + 2, cut)
+    cut_a = (y + 2) // 3
+    cut_b = cut_a + (y - cut_a + 1) // 2
+    near_loop(0, cut_a)
     far_loop(9, 2)
     pump(6, 0)
     pump(6, 1)
     k_columns(11, 2)
-    near_loop(cut, PLANE // 4)
-    for s in range(PLANE):
-        q_out[s] = jnp.max(acc_q[:, s * R:(s + 1) * R], axis=0, keepdims=True)
+    near_loop(cut_a, cut_b)
+    far_loop(11, 2)
     pump(7, 0)
     pump(7, 1)
-    for k in range(1, PLANE):
-        go(reply(k))
-    far_loop(11, 2)
+    near_loop(cut_b, y)
+    for s in range(NEAR_SLOTS):
+        k_out[s] = jnp.max(acc_k[s * R:(s + 1) * R, :].T, axis=0, keepdims=True)
+    for s in range(1, NEAR_SLOTS):
+        go(back(s))
     k_columns(13, 2)
     far_loop(13, 2)
-    send_back(9, 6)
-    best = q_out[me]
+    pump(8, 0)
+    k_columns(15, 1)
+    far_loop(15, 1)
+    for k in sorted(range(1, PLANE), key=hops, reverse=True):
+        s, result = plane_result(k)
+        q_out[s] = result
+        go(reply(k))
+    best = jnp.maximum(k_out[0], plane_result(0)[1])
+    for s in range(1, NEAR_SLOTS):
+        rc(k_out.at[0], k_in.at[s], ns.at[0], nr.at[s], dev(dz=1)).wait_recv()
+    for s in range(1, NEAR_SLOTS):
+        best = jnp.maximum(best, k_in[s])
     for k in range(1, PLANE):
         reply(k).wait_recv()
     for k in range(1, PLANE):
         best = jnp.maximum(best, q_in[k])
-    pump(8, 0)
-    k_columns(15, 1)
-    far_loop(15, 1)
-    send_back(15, 1)
-    for s in range(FAR_SLOTS):
-        rc(k_out.at[0], k_in.at[s], ns.at[0], nr.at[s], dev(dz=1)).wait_recv()
-    for s in range(FAR_SLOTS):
-        best = jnp.maximum(best, k_in[s])
     out_ref[...] = best
     for copy in pending:
         copy.wait_send()
@@ -400,16 +404,16 @@
                 pltpu.VMEM((NZ * R, R), f32),
                 pltpu.VMEM((NZ * R, R), f32),
                 pltpu.VMEM((8, PLANE * R), f32),
-                pltpu.VMEM((FAR_SLOTS * R, R), f32),
-                pltpu.VMEM((FAR_SLOTS, 1, R), f32),
-                pltpu.VMEM((FAR_SLOTS, 1, R), f32),
+                pltpu.VMEM((NEAR_SLOTS * R, R), f32),
+                pltpu.VMEM((NEAR_SLOTS, 1, R), f32),
+                pltpu.VMEM((NEAR_SLOTS, 1, R), f32),
                 pltpu.VMEM((PLANE, 1, R), f32),
                 pltpu.VMEM((PLANE, 1, R), f32),
                 dma((3,)),
                 dma((2 * sum(CHUNKS),)), dma((2 * sum(CHUNKS),)), dma((NZ,)), dma((NZ,)),
                 dma((40,)), dma((40,)), dma((15,)), dma((15,)),
                 dma((16,)), dma((16,)), dma((16,)), dma((16,)),
-                dma((FAR_SLOTS,)), dma((FAR_SLOTS,)), dma((PLANE,)), dma((PLANE,)),
+                dma((NEAR_SLOTS,)), dma((NEAR_SLOTS,)), dma((PLANE,)), dma((PLANE,)),
             ],
             compiler_params=pltpu.CompilerParams(
                 collective_id=0, has_side_effects=True, vmem_limit_bytes=60 * 2**20),

time: 59.6 us -> 57 us (0.956)
  the two profiles are of different devices: /device:TPU:24 before, /device:TPU:1 now
where the time goes in v5:
time: 57 us; the launch traced here: 56.9 us
  Pallas kernels  55.8 us (98%)
  local copies, waits for them, and re-layouts  1.1 us (2%)
    pallas_call x1, Pallas kernels, step(): pl.pallas_call(kernel, out_shape=jax.ShapeDtypeStruct((1, R), f32), in_sp...  55.8 us

profile of v5, /device:TPU:1, one launch (start us, length us, event | category | flops | bytes accessed | tf_op | source)
XLA Modules:
  0.0 56.9 jit_solution(5283178939608925728)
XLA Ops:
  0.0 55.8 %shard_map.37 = f32[1,128]{1,0:T(1,128)} custom-call(bf16[128,512]{1,0:T(8,128)(2,1)} %emb_hbm.1, s32[1,128]{1,0:T(1,128)} %bitcast.4, s32[1,256]{1,0:T(1,128)} %bitcast.3), custom_call_target="tpu_custom_call" | custom-call | tf_op jit(solution)/shard_map/pallas_call | solution.py:391
  55.8 0.0 copy-start
  55.8 0.6 %copy-done = f32[1,128]{1,0:T(1,128)S(1)} copy-done((f32[1,128]{1,0:T(1,128)S(1)}, f32[1,128]{1,0:T(1,128)}, u32[]{:S(2)}) %copy-start) | copy-done | bytes 536
  56.4 0.5 copy.5
Async XLA Ops:
  55.8 0.6 %copy-start = (f32[1,128]{1,0:T(1,128)S(1)}, f32[1,128]{1,0:T(1,128)}, u32[]{:S(2)}) copy-start(f32[1,128]{1,0:T(1,128)} %shard_map.37) | copy-start | bytes 1540

commit v6 on v5

--- a/solution.py
+++ b/solution.py
@@ -210,13 +210,13 @@
     own_share[1].wait_recv()
     go(ring_meta(1, 1))
     pump(1, 0)
-    pump(1, 1)
     line(-1)
     line(1)
-    pump(2, 0)
+    pump(1, 1)
     cross(0)
     for dx, dy in ((-1, 0), (1, 0), (0, -1), (0, 1)):
         give(dx, dy)
+    pump(2, 0)
     pump(2, 1)
     for h in range(2):
         for sign in ("+", "-"):

time: 57 us -> 56.5 us (level)
  Pallas kernels: 55.8 us -> 55.2 us
where the time goes in v6:
time: 56.5 us; the launch traced here: 56.3 us
  Pallas kernels  55.2 us (98%)
  local copies, waits for them, and re-layouts  1.1 us (2%)
    pallas_call x1, Pallas kernels, step(): pl.pallas_call(kernel, out_shape=jax.ShapeDtypeStruct((1, R), f32), in_sp...  55.2 us

profile of v6, /device:TPU:1, one launch (start us, length us, event | category | flops | bytes accessed | tf_op | source)
XLA Modules:
  0.0 56.3 jit_solution(11405437295859915446)
XLA Ops:
  0.0 55.2 %shard_map.37 = f32[1,128]{1,0:T(1,128)} custom-call(bf16[128,512]{1,0:T(8,128)(2,1)} %emb_hbm.1, s32[1,128]{1,0:T(1,128)} %bitcast.4, s32[1,256]{1,0:T(1,128)} %bitcast.3), custom_call_target="tpu_custom_call" | custom-call | tf_op jit(solution)/shard_map/pallas_call | solution.py:391
  55.2 0.0 copy-start
  55.2 0.6 %copy-done = f32[1,128]{1,0:T(1,128)S(1)} copy-done((f32[1,128]{1,0:T(1,128)S(1)}, f32[1,128]{1,0:T(1,128)}, u32[]{:S(2)}) %copy-start) | copy-done | bytes 536
  55.8 0.5 copy.5
Async XLA Ops:
  55.2 0.6 %copy-start = (f32[1,128]{1,0:T(1,128)S(1)}, f32[1,128]{1,0:T(1,128)}, u32[]{:S(2)}) copy-start(f32[1,128]{1,0:T(1,128)} %shard_map.37) | copy-start | bytes 1540

commit v7 on v6

--- a/solution.py
+++ b/solution.py
@@ -217,7 +217,6 @@
     for dx, dy in ((-1, 0), (1, 0), (0, -1), (0, 1)):
         give(dx, dy)
     pump(2, 0)
-    pump(2, 1)
     for h in range(2):
         for sign in ("+", "-"):
             move(h, 0, 0, "f" + sign).wait_recv()
@@ -227,6 +226,7 @@
     for h in range(2):
         go(move(h, 1, 2, "+"))
         go(move(h, 1, 2, "-"))
+    pump(2, 1)
     cross(-1)
     pump(3, 0)
     cross(1)

time: 56.5 us -> 57.7 us (1.021)
  Pallas kernels: 55.2 us -> 56.4 us
    pallas_call x1, Pallas kernels: 55.2 us -> 56.4 us  [step(): pl.pallas_call(kernel, out_shape=jax.ShapeDtypeStruct((1, R), f32), in_sp...]
where the time goes in v7:
time: 57.7 us; the launch traced here: 57.6 us
  Pallas kernels  56.4 us (98%)
  local copies, waits for them, and re-layouts  1.1 us (2%)
    pallas_call x1, Pallas kernels, step(): pl.pallas_call(kernel, out_shape=jax.ShapeDtypeStruct((1, R), f32), in_sp...  56.4 us

profile of v7, /device:TPU:1, one launch (start us, length us, event | category | flops | bytes accessed | tf_op | source)
XLA Modules:
  0.0 57.6 jit_solution(538316813322890868)
XLA Ops:
  0.0 56.4 %shard_map.37 = f32[1,128]{1,0:T(1,128)} custom-call(bf16[128,512]{1,0:T(8,128)(2,1)} %emb_hbm.1, s32[1,128]{1,0:T(1,128)} %bitcast.4, s32[1,256]{1,0:T(1,128)} %bitcast.3), custom_call_target="tpu_custom_call" | custom-call | tf_op jit(solution)/shard_map/pallas_call | solution.py:391
  56.4 0.0 copy-start
  56.5 0.6 %copy-done = f32[1,128]{1,0:T(1,128)S(1)} copy-done((f32[1,128]{1,0:T(1,128)S(1)}, f32[1,128]{1,0:T(1,128)}, u32[]{:S(2)}) %copy-start) | copy-done | bytes 536
  57.0 0.5 copy.5
Async XLA Ops:
  56.4 0.6 %copy-start = (f32[1,128]{1,0:T(1,128)S(1)}, f32[1,128]{1,0:T(1,128)}, u32[]{:S(2)}) copy-start(f32[1,128]{1,0:T(1,128)} %shard_map.37) | copy-start | bytes 1540
